TPU v7x, 512 devices: a whole 4x8x8 slice. The times are simulated.
512 devices in a mesh: wide: 32 (over y, x_hi, core), narrow: 8 (over z), act: 2 (over x_lo).
Axes of the slice: x: 4 (x_hi: 2, x_lo: 2; x = x_hi * 2 + x_lo), y: 8, z: 8, core: 2. Of those that a mesh axis runs over, the one named last changes fastest.
Arguments:
- value_now: float32 [64, 64, 128, 128], P('wide', 'narrow'), may hold values from -8 to 8, as said below
- cost_first: float32 [8, 64], replicated, may hold values from -6 to 332, as said below
- cost_second: float32 [8, 64], replicated, may hold values from -6 to 6
- cost_third: float32 [8, 128], replicated, may hold values from -6 to 6
- cost_fourth: float32 [8, 128], replicated, may hold values from -6 to 6
- trans_weights: float32 [8, 4, 65], replicated, may hold values from 0.0001 to 1
- trans_offsets: int32 [8, 4], replicated, may hold values from -32 to 32
- action_order: int32 [8], replicated, may hold values from 0 to 7, each once
Outputs:
- new_value: float32 [64, 64, 128, 128], P('wide', 'narrow')
- choice_prob: bfloat16 [8, 64, 64, 128, 128], P('act', 'wide', 'narrow')
Inputs may be any that keep to these rules, and one draw needn't show every extreme that they name: `value_now`: A value function of order one with rough and broad variation. `cost_first`: flow utility terms of order one in most entries.
All inputs are finite; a program needn't handle non-finite values.
Results may differ from a plain program's by a relative error of at most 0.001.
Values sent between devices are 32-bit elements; how exact they have to be, the bound alone decides.
A program may use at most 64 MiB of HBM per device.

v0:
```python
import jax
import jax.numpy as jnp
from jax import lax
from jax.sharding import PartitionSpec as P

DISCOUNT = 0.95
HIGHEST = lax.Precision.HIGHEST


def merged(value, axis, join):
    pieces = jax.tree.map(lambda part: lax.all_gather(part, axis), value)
    head = jax.tree.map(lambda part: part[0], pieces)
    tail = jax.tree.map(lambda part: part[1:], pieces)
    subtotal, _ = lax.scan(lambda subtotal, slab: (join(subtotal, slab), None), head, tail)
    return subtotal


def transition(weights, offset, length):
    band_len = weights.shape[0]
    half_band = (band_len - 1) // 2
    normed = weights / jnp.sum(weights)
    row_ids = jnp.arange(length, dtype=jnp.int32)
    tap_ids = jnp.arange(band_len, dtype=jnp.int32)
    target = jnp.clip(row_ids[:, None] + offset + tap_ids[None, :] - half_band, 0, length - 1)
    matched = (target[:, :, None] == row_ids[None, None, :]).astype(normed.dtype)
    return jnp.einsum("ijk,j->ik", matched, normed, precision=HIGHEST)


def merge_pair(first_pair, second_pair):
    top_score = jnp.maximum(first_pair[0], second_pair[0])
    summed = first_pair[1] * jnp.exp(first_pair[0] - top_score) + second_pair[1] * jnp.exp(
        second_pair[0] - top_score
    )
    return (top_score, summed)


def body(
    value_now,
    cost_first,
    cost_second,
    cost_third,
    cost_fourth,
    trans_weights,
    trans_offsets,
    action_order,
):
    size_act = lax.axis_size("act")
    per_group = action_order.shape[0] // size_act
    group_id = lax.axis_index("act")
    my_actions = lax.dynamic_slice_in_dim(action_order, group_id * per_group, per_group)
    rows_first, rows_second, len_third, len_fourth = value_now.shape
    len_first = rows_first * lax.axis_size("wide")
    len_second = rows_second * lax.axis_size("narrow")
    my_weights = jnp.take(trans_weights, my_actions, axis=0)
    my_offsets = jnp.take(trans_offsets, my_actions, axis=0)

    def build(axis_id, length):
        return jax.vmap(lambda weight_row, offset_one: transition(weight_row, offset_one, length))(
            my_weights[:, axis_id], my_offsets[:, axis_id]
        )

    mat_first = build(0, len_first)
    mat_second = build(1, len_second)
    mat_third = build(2, len_third)
    mat_fourth = build(3, len_fourth)
    spread = lax.all_to_all(value_now, "narrow", split_axis=2, concat_axis=1, tiled=True)
    field = jnp.einsum("gij,ajcd->gaicd", mat_second, spread, precision=HIGHEST)
    field = jnp.einsum("gij,gabcj->gabci", mat_fourth, field, precision=HIGHEST)
    field = lax.all_to_all(field, "narrow", split_axis=2, concat_axis=3, tiled=True)
    field = lax.all_to_all(field, "wide", split_axis=3, concat_axis=1, tiled=True)
    field = jnp.einsum("gij,gjbcd->gibcd", mat_first, field, precision=HIGHEST)
    field = lax.all_to_all(field, "wide", split_axis=1, concat_axis=3, tiled=True)
    expected = jnp.einsum("gij,gabjd->gabid", mat_third, field, precision=HIGHEST)
    start_first = lax.axis_index("wide") * rows_first
    start_second = lax.axis_index("narrow") * rows_second
    util_first = lax.dynamic_slice_in_dim(
        jnp.take(cost_first, my_actions, axis=0), start_first, rows_first, 1
    )
    util_second = lax.dynamic_slice_in_dim(
        jnp.take(cost_second, my_actions, axis=0), start_second, rows_second, 1
    )
    util_third = jnp.take(cost_third, my_actions, axis=0)
    util_fourth = jnp.take(cost_fourth, my_actions, axis=0)
    utility = (
        util_first[:, :, None, None, None]
        + util_second[:, None, :, None, None]
        + util_third[:, None, None, :, None]
        + util_fourth[:, None, None, None, :]
    )
    scores = utility + DISCOUNT * expected
    local_max = jnp.max(scores, axis=0)
    local_sum = jnp.sum(jnp.exp(scores - local_max), axis=0)
    total_max, total_sum = merged((local_max, local_sum), "act", merge_pair)
    log_total = total_max + jnp.log(total_sum)
    choice_prob = jnp.exp(scores - log_total).astype(jnp.bfloat16)
    return (log_total, choice_prob)


def solution(mesh):
    return jax.shard_map(
        body,
        mesh=mesh,
        in_specs=(P("wide", "narrow", None, None), P(), P(), P(), P(), P(), P(), P()),
        out_specs=(P("wide", "narrow", None, None), P("act", "wide", "narrow", None, None)),
        check_vma=False,
    )
```

profile of v0, /device:TPU:1, one launch (start us, length us, event | category | flops | bytes accessed | tf_op | source)
XLA Modules:
  0.0 500.8 jit_solution(10567175527242536699)
XLA Ops:
  7.2 2.8 copy.94
  10.0 10.9 %all-to-all-start = ((f32[2,8,128,128]{3,1,0,2:T(8,128)}), f32[2,8,128,128]{3,1,0,2:T(8,128)S(1)}, u32[]{:S(2)}, u32[]{:S(2)}) async-start(f32[2,8,128,128]{3,1,0,2:T(8,128)} %copy.94), calls=%async_computation | async-start | bytes 2097152 | tf_op jit(solution)/shard_map/all_to_all | solution.py:66
  20.9 0.1 compare_and_fusion
  21.0 0.1 copy.93
  21.1 0.6 gather_fusion
  21.7 0.2 slice_reduce_fusion.2
  21.9 0.6 gather_fusion.1
  22.6 0.1 slice_reduce_fusion.6
  22.8 0.1 add_clamp_fusion.2
  23.1 7.0 %fusion.5 = f32[4,1,64,64]{3,1,2,0:T(1,128)S(1)} fusion(f32[4,65,1,1]{1,2,3,0:T(1,128)S(1)} %bitcast.128, s32[4,64,65]{2,1,0:T(8,128)S(1)} %add_clamp_fusion.2), kind=kOutput, calls=%fused_computation.15 | convolution fusion | flops 13844480 | bytes 133136 | tf_op jit(solution)/shard_map/vmap(ijk,j->ik)/dot_general | solution.py:26
  30.2 6.7 %iota_compare_fusion.1 = pred[4,128,65,128]{3,1,2,0:T(32,128)(4,1)S(1)} fusion(s32[4,128,65]{1,2,0:T(8,128)S(1)} %add_clamp_fusion.1), kind=kLoop, calls=%fused_computation.11 | loop fusion | flops 4259840 | bytes 4392960 | tf_op jit(solution)/shard_map/vmap()/eq | solution.py:25
  36.9 9.3 %fusion.2 = f32[4,1,128,128]{3,1,2,0:T(1,128)S(1)} fusion(f32[4,65,1,1]{1,2,3,0:T(1,128)S(1)} %bitcast.129, pred[4,128,65,128]{3,1,2,0:T(32,128)(4,1)S(1)} %iota_compare_fusion.1), kind=kOutput, calls=%fused_computation.8 | convolution fusion | flops 51118080 | bytes 4523024 | tf_op jit(solution)/shard_map/vmap(ijk,j->ik)/dot_general | solution.py:26
  46.2 3.9 all-to-all-done
  50.1 0.3 copy.96
  50.4 3.9 convolution_bitcast_fusion
  54.3 6.8 %fusion.8 = f32[4,2,64,16,128]{4,3,1,0,2:T(8,128)S(1)} fusion(f32[4,128,128,1,1]{2,1,3,0,4:T(8,128)S(1)} %bitcast.119, f32[4,2,64,16,128]{4,2,3,1,0:T(8,128)S(1)} %convolution_bitcast_fusion), kind=kOutput, calls=%fused_computation.19 | convolution fusion | flops 1610612736 | bytes 8650752 | tf_op jit(solution)/shard_map/gij,gabcj->gabci/dot_general | solution.py:68
  61.2 96.6 %all_to_all.72 = f32[4,2,64,16,128]{4,3,1,0,2:T(8,128)S(1)} all-to-all(f32[4,2,64,16,128]{4,3,1,0,2:T(8,128)S(1)} %fusion.8), channel_id=1, replica_groups=mesh['wide'=32,'narrow'=8,'act'=2] {'narrow'}, dimensions={2} | all-to-all | bytes 8388608 | tf_op jit(solution)/shard_map/all_to_all | solution.py:69
  157.7 0.6 copy.101
  158.3 4.4 copy.102
  162.7 13.2 %all-to-all-start.2 = ((f32[4,2,8,128,128]{4,2,1,0,3:T(8,128)}), f32[4,2,8,128,128]{4,2,1,0,3:T(8,128)}, u32[]{:S(2)}, u32[]{:S(2)}) async-start(f32[4,2,8,128,128]{4,2,1,0,3:T(8,128)} %copy.102), calls=%async_computation.2 | async-start | bytes 8388608 | tf_op jit(solution)/shard_map/all_to_all | solution.py:70
  176.0 0.1 add_clamp_fusion.3
  176.1 7.1 %fusion.4 = f32[4,1,64,64]{3,1,2,0:T(1,128)S(1)} fusion(f32[4,65,1,1]{1,2,3,0:T(1,128)S(1)} %bitcast.127, s32[4,64,65]{2,1,0:T(8,128)S(1)} %add_clamp_fusion.3), kind=kOutput, calls=%fused_computation.14 | convolution fusion | flops 13844480 | bytes 133136 | tf_op jit(solution)/shard_map/vmap(ijk,j->ik)/dot_general | solution.py:26
  183.2 86.7 %all-to-all-done.2 = f32[4,2,8,128,128]{4,2,1,0,3:T(8,128)} async-done(((f32[4,2,8,128,128]{4,2,1,0,3:T(8,128)}), f32[4,2,8,128,128]{4,2,1,0,3:T(8,128)}, u32[]{:S(2)}, u32[]{:S(2)}) %all-to-all-start.2) | async-done | bytes 4194336 | tf_op jit(solution)/shard_map/all_to_all | solution.py:70
  269.8 4.3 copy.104
  274.2 4.0 fusion.24
  278.2 4.7 copy.105
  282.9 7.6 %all-to-all-start.3 = ((f32[4,64,8,4,128]{4,3,2,0,1:T(4,128)}), f32[4,64,8,4,128]{4,3,2,0,1:T(4,128)}, u32[]{:S(2)}, u32[]{:S(2)}) async-start(f32[4,64,8,4,128]{4,3,2,0,1:T(4,128)} %copy.105), calls=%async_computation.3 | async-start | bytes 8388608 | tf_op jit(solution)/shard_map/all_to_all | solution.py:72
  290.6 0.6 gather_fusion.5
  291.2 0.6 gather_fusion.4
  291.7 0.6 gather_fusion.3
  292.3 0.6 gather_fusion.2
  293.3 6.9 %iota_compare_fusion = pred[4,128,65,128]{3,1,2,0:T(32,128)(4,1)S(1)} fusion(s32[4,128,65]{1,2,0:T(8,128)S(1)} %add_clamp_fusion), kind=kLoop, calls=%fused_computation.10 | loop fusion | flops 4259840 | bytes 4392960 | tf_op jit(solution)/shard_map/vmap()/eq | solution.py:25
  300.3 9.3 %fusion = f32[4,1,128,128]{3,1,2,0:T(1,128)S(1)} fusion(f32[4,65,1,1]{1,2,3,0:T(1,128)S(1)} %bitcast.126, pred[4,128,65,128]{3,1,2,0:T(32,128)(4,1)S(1)} %iota_compare_fusion), kind=kOutput, calls=%fused_computation.6 | convolution fusion | flops 51118080 | bytes 4523024 | tf_op jit(solution)/shard_map/vmap(ijk,j->ik)/dot_general | solution.py:26
  309.5 75.1 %all-to-all-done.3 = f32[4,64,8,4,128]{4,3,2,0,1:T(4,128)} async-done(((f32[4,64,8,4,128]{4,3,2,0,1:T(4,128)}), f32[4,64,8,4,128]{4,3,2,0,1:T(4,128)}, u32[]{:S(2)}, u32[]{:S(2)}) %all-to-all-start.3) | async-done | bytes 4194336 | tf_op jit(solution)/shard_map/all_to_all | solution.py:72
  384.6 2.8 copy.106
  387.4 0.6 copy.107
  388.0 7.6 %fusion.12 = (f32[2,8,128,128]{2,3,1,0:T(8,128)S(1)}, f32[4,2,8,128,128]{4,3,2,1,0:T(8,128)S(1)}) fusion(f32[4,128]{1,0:T(4,128)S(1)} %get-tuple-element.50, f32[4,2,8,128]{3,2,1,0:T(8,128)S(1)} %broadcast_add_fusion, f32[4,128,128,1,1]{2,1,4,3,0:T(8,128)S(1)} %bitcast.118, f32[4,2,8,128,128]{4,2,3,1,0:T(8,128)S(1)} %bitcast.111), kind=kOutput, calls=%fused_computation.25 | convolution fusion | flops 1614544896 | bytes 9734144 | tf_op jit(solution)/shard_map/gij,gabjd->gabid/dot_general | solution.py:73
  395.6 1.9 copy-done.2
  397.5 1.1 exponential_reduce_fusion
  398.7 1.3 copy.110
  400.1 1.3 copy.109
  401.4 32.8 %all-gather.7.cloned.1.call-done = f32[4,8,128,128]{3,2,1,0:T(8,128)} async-done(((f32[2,8,128,128]{3,2,1,0:T(8,128)}), f32[4,8,128,128]{3,2,1,0:T(8,128)}) %all-gather.7.cloned.1.call-update) | async-done | bytes 2097168 | tf_op jit(solution)/shard_map/all_gather | solution.py:11
  434.2 44.7 %all-gather.5.cloned.1.call-done = f32[4,8,128,128]{3,2,1,0:T(8,128)} async-done(((f32[2,8,128,128]{3,2,1,0:T(8,128)}), f32[4,8,128,128]{3,2,1,0:T(8,128)}) %all-gather.5.cloned.1.call-update) | async-done | bytes 2097168 | tf_op jit(solution)/shard_map/all_gather | solution.py:11
  478.8 2.6 fusion.16
  481.5 0.3 copy.111
  481.8 4.8 exponential_convert_fusion
  486.6 3.9 copy.112
  490.5 3.0 log_add_fusion
  (38 shorter events, 1.1 us)
Async XLA Ops:
  7.2 14.8 %copy-start = (f32[8,4,65]{2,1,0:T(4,128)S(1)}, f32[8,4,65]{2,1,0:T(4,128)}, u32[]{:S(2)}) copy-start(f32[8,4,65]{2,1,0:T(4,128)} %param.17) | copy-start | bytes 24964
  7.2 13.7 %copy-start.9 = (s32[8]{0:T(128)S(1)}, s32[8]{0:T(128)}, u32[]{:S(2)}) copy-start(s32[8]{0:T(128)} %param.19) | copy-start | bytes 100
  7.2 13.8 %copy-start.8 = (s32[8,4]{0,1:T(4,128)S(1)}, s32[8,4]{0,1:T(4,128)}, u32[]{:S(2)}) copy-start(s32[8,4]{0,1:T(4,128)} %param.18) | copy-start | bytes 388
  10.0 40.0 %all-to-all-start = ((f32[2,8,128,128]{3,1,0,2:T(8,128)}), f32[2,8,128,128]{3,1,0,2:T(8,128)S(1)}, u32[]{:S(2)}, u32[]{:S(2)}) async-start(f32[2,8,128,128]{3,1,0,2:T(8,128)} %copy.94), calls=%async_computation | async-start | bytes 2097152 | tf_op jit(solution)/shard_map/all_to_all | solution.py:66
  162.7 107.1 %all-to-all-start.2 = ((f32[4,2,8,128,128]{4,2,1,0,3:T(8,128)}), f32[4,2,8,128,128]{4,2,1,0,3:T(8,128)}, u32[]{:S(2)}, u32[]{:S(2)}) async-start(f32[4,2,8,128,128]{4,2,1,0,3:T(8,128)} %copy.102), calls=%async_computation.2 | async-start | bytes 8388608 | tf_op jit(solution)/shard_map/all_to_all | solution.py:70
  282.9 7.7 %copy-start.4 = (f32[8,128]{1,0:T(8,128)S(1)}, f32[8,128]{1,0:T(8,128)}, u32[]{:S(2)}) copy-start(f32[8,128]{1,0:T(8,128)} %param.16) | copy-start | bytes 12292
  282.9 8.3 %copy-start.5 = (f32[8,128]{1,0:T(8,128)S(1)}, f32[8,128]{1,0:T(8,128)}, u32[]{:S(2)}) copy-start(f32[8,128]{1,0:T(8,128)} %param.15) | copy-start | bytes 12292
  282.9 8.8 %copy-start.6 = (f32[8,64]{1,0:T(8,128)S(1)}, f32[8,64]{1,0:T(8,128)}, u32[]{:S(2)}) copy-start(f32[8,64]{1,0:T(8,128)} %param.14) | copy-start | bytes 6148
  282.9 9.4 %copy-start.7 = (f32[8,64]{1,0:T(8,128)S(1)}, f32[8,64]{1,0:T(8,128)}, u32[]{:S(2)}) copy-start(f32[8,64]{1,0:T(8,128)} %param.13) | copy-start | bytes 6148
  282.9 101.7 %all-to-all-start.3 = ((f32[4,64,8,4,128]{4,3,2,0,1:T(4,128)}), f32[4,64,8,4,128]{4,3,2,0,1:T(4,128)}, u32[]{:S(2)}, u32[]{:S(2)}) async-start(f32[4,64,8,4,128]{4,3,2,0,1:T(4,128)} %copy.105), calls=%async_computation.3 | async-start | bytes 8388608 | tf_op jit(solution)/shard_map/all_to_all | solution.py:72
  290.5 143.7 %all-gather.7.cloned.1.call-start = ((), (), s32[]{:S(2)}) async-start(), calls=%async_computation.5 | async-start | bytes 3145728 | tf_op jit(solution)/shard_map/all_gather | solution.py:11
  395.6 1.9 copy-start.2
  400.0 78.8 %all-gather.5.cloned.1.call-start = ((), (), s32[]{:S(2)}) async-start(), calls=%async_computation.4 | async-start | bytes 3145728 | tf_op jit(solution)/shard_map/all_gather | solution.py:11
  481.8 8.7 %copy-start.3 = (f32[4,8,128,128]{3,2,1,0:T(8,128)S(1)}, f32[4,8,128,128]{3,2,1,0:T(8,128)}, u32[]{:S(2)}) copy-start(f32[4,8,128,128]{3,2,1,0:T(8,128)} %all-gather.7.cloned.1.call-done) | copy-start | bytes 6291460
  481.8 11.7 %copy-start.1 = (f32[8,4,65]{2,1,0:T(4,128)S(1)}, f32[8,4,65]{2,1,0:T(4,128)}, u32[]{:S(2)}) copy-start(f32[8,4,65]{2,1,0:T(4,128)} %param.17) | copy-start | bytes 24964
Sparse Core Ops, SparseCore 0:
  400.1 33.9 all-gather.6
  436.8 41.9 all-gather.4
where the time goes:
time: 511 us; the launch traced here: 501 us
  waiting for transfers between devices  243 us (48%)
  blocking collectives  96.6 us (19%)
  matrix products  55 us (11%)
  local copies, waits for them, and re-layouts  33.2 us (6%)
  starting transfers between devices  31.8 us (6%)
  other arithmetic  26.3 us (5%)
  between operations  14.8 us (3%)
    all_to_all x1, blocking collectives, body(): lax.all_to_all(field, 'narrow', split_axis=2, concat_axis=3, tiled=True)  96.6 us
    all_to_all x1, waiting for transfers between devices, body(): lax.all_to_all(field, 'wide', split_axis=3, concat_axis=1, tiled=True)  86.7 us
    all_gather x2, waiting for transfers between devices, merged(): pieces = jax.tree.map(lambda part: lax.all_gather(part, axis), value)  77.5 us
    all_to_all x1, waiting for transfers between devices, body(): lax.all_to_all(field, 'wide', split_axis=1, concat_axis=3, tiled=True)  75.1 us
    dot_general x4, matrix products, transition(): return jnp.einsum('ijk,j->ik', matched, normed, precision=HIGHEST)  32.7 us
    eq x2, other arithmetic, transition(): target[:, :, None] == row_ids[None, None, :]  13.6 us
    all_to_all x1, starting transfers between devices, body(): lax.all_to_all(field, 'wide', split_axis=3, concat_axis=1, tiled=True)  13.2 us
    all_to_all x1, starting transfers between devices, body(): lax.all_to_all(value_now, 'narrow', split_axis=2, concat_axis=1, tiled=True)  10.9 us
  transfers between devices with their start and end apart: 5, of which 5 were waited for; matrix products, arithmetic and copies ran while one was open for 11% of the time, Pallas kernels for 0%

commit v1 on v0

v1 whole, which is shorter than its diff:
```python
import jax
import jax.numpy as jnp
from jax import lax
from jax.experimental import pallas as pl
from jax.experimental.pallas import tpu as pltpu
from jax.sharding import PartitionSpec as P

DISCOUNT = 0.95
MESH = pl.DeviceIdType.MESH
F32 = jnp.float32
BF16 = jnp.bfloat16
VMEM = pl.BlockSpec(memory_space=pltpu.VMEM)
SMEM = pl.BlockSpec(memory_space=pltpu.SMEM)
LIMIT = 56 * 1024 * 1024


def place():
    wide = lax.axis_index("wide")
    return lax.div(wide, 4), lax.rem(wide, 4), lax.axis_index("narrow"), lax.axis_index("act")


def partner(step, t, q):
    return lax.rem(t + lax.div(step, 4), 8), lax.rem(q + lax.rem(step, 4), 4)


def halves(x):
    high = x.astype(BF16)
    low = (x - high.astype(F32)).astype(BF16)
    return high, low


def build_kernel(order_ref, offs_ref, w_ref, c0_ref, c1_ref, w2_ref, w3_ref):
    act = lax.axis_index("act")

    def toeplitz(a, d, length):
        row = w_ref[pl.ds(a, 1), d, :]
        row = row / jnp.sum(row)
        shift = lax.rem(offs_ref[a, d] - 32 + 256, 256)
        spread = jnp.broadcast_to(pltpu.roll(jnp.broadcast_to(row, (8, 256)), shift, 1)[0:1], (length, 256))
        number = lax.broadcasted_iota(jnp.int32, (length, 256), 0)
        lane = lax.broadcasted_iota(jnp.int32, (length, 256), 1)
        bit = 1
        while bit < length:
            spread = jnp.where(lax.rem(lax.div(number, bit), 2) == 1, pltpu.roll(spread, bit, 1), spread)
            bit *= 2
        zero = jnp.zeros_like(spread)
        below = jnp.sum(jnp.where(lane >= 192, spread, zero), axis=1, keepdims=True)
        above = jnp.sum(jnp.where((lane >= length) & (lane < 192), spread, zero), axis=1, keepdims=True)
        full = jnp.where(lane == 0, spread + below, jnp.where(lane == length - 1, spread + above, spread))
        full = jnp.where(lane < length, full, zero)
        high = full.astype(BF16).astype(F32)
        return high, full - high

    def one(j, carry):
        a = order_ref[j]
        for d, ref in ((0, c0_ref), (1, c1_ref)):
            high, low = toeplitz(a, d, 64)
            both = high + pltpu.roll(high, 64, 1) + pltpu.roll(low, 128, 1)
            ref[0, j] = both[:, :128]
            ref[1, j] = both[:, 128:]
        return carry

    lax.fori_loop(0, 8, one, 0)

    def mine(j, carry):
        a = order_ref[act * 4 + j]
        for d, ref in ((2, w2_ref), (3, w3_ref)):
            high, low = toeplitz(a, d, 128)
            ref[j, :, 0:128] = high[:, :128].astype(BF16)
            ref[j, :, 128:256] = high[:, :128].astype(BF16)
            ref[j, :, 256:384] = low[:, :128].astype(BF16)
        return carry

    lax.fori_loop(0, 4, mine, 0)


def build(order, offsets, weights):
    padded = jnp.pad(weights, ((0, 0), (0, 0), (0, 256 - weights.shape[2])))
    return pl.pallas_call(
        build_kernel,
        out_shape=(
            jax.ShapeDtypeStruct((2, 8, 64, 128), F32),
            jax.ShapeDtypeStruct((2, 8, 64, 128), F32),
            jax.ShapeDtypeStruct((4, 128, 384), BF16),
            jax.ShapeDtypeStruct((4, 128, 384), BF16),
        ),
        in_specs=[SMEM, SMEM, VMEM],
        out_specs=(VMEM,) * 4,
        name="build",
    )(order, offsets, padded)


def spread_kernel(vt_ref, ga_ref, gb_ref, send_sem, recv_sem, local_sem, ring_send, ring_recv):
    y, q, z, act = place()
    wide = 4 * y + q
    barrier = pltpu.get_barrier_semaphore()

    def at_a(step):
        t, p = partner(step, y, q)
        return t * 8 + p * 2 + act, {"wide": 4 * t + p, "narrow": z, "act": act}

    def at_b(step):
        t, p = partner(step, z, q)
        return 64 + t * 8 + p * 2 + act, {"wide": 4 * y + p, "narrow": t, "act": act}

    def greet(step, carry):
        pl.semaphore_signal(barrier, inc=1, device_id=at_a(step)[1], device_id_type=MESH)
        pl.semaphore_signal(barrier, inc=1, device_id=at_b(step)[1], device_id_type=MESH)
        return carry

    lax.fori_loop(1, 32, greet, 0)
    own = [
        pltpu.make_async_copy(vt_ref.at[y * 8 + q * 2 + act], ga_ref.at[z, wide], local_sem.at[0]),
        pltpu.make_async_copy(vt_ref.at[64 + z * 8 + q * 2 + act], gb_ref.at[y, 4 * z + q], local_sem.at[1]),
    ]
    for copy in own:
        copy.start()
    pl.semaphore_wait(barrier, 62)

    def send(step, carry):
        row, device = at_a(step)
        pltpu.make_async_remote_copy(
            vt_ref.at[row], ga_ref.at[z, wide], send_sem.at[0], recv_sem.at[0], device, MESH
        ).start()
        row, device = at_b(step)
        pltpu.make_async_remote_copy(
            vt_ref.at[row], gb_ref.at[y, 4 * z + q], send_sem.at[1], recv_sem.at[1], device, MESH
        ).start()
        return carry

    lax.fori_loop(1, 32, send, 0)
    for copy in own:
        copy.wait()
    streams = (
        (ga_ref, z, lambda t: {"wide": wide, "narrow": t, "act": act}),
        (gb_ref, y, lambda t: {"wide": 4 * t + q, "narrow": z, "act": act}),
    )
    for index, (ref, _, _) in enumerate(streams):
        part = ref.at[0, pl.ds(0, 31)]
        pltpu.make_async_copy(part, part, recv_sem.at[index]).wait()

    def hop(index, step, half, way):
        ref, t, device = streams[index]
        block = lax.rem(t + 8 - way * (step - 1), 8)
        piece = ref.at[block, pl.ds(16 * half, 16)]
        side = 0 if way > 0 else 1
        return pltpu.make_async_remote_copy(
            piece,
            piece,
            ring_send.at[index, step - 1, half, side],
            ring_recv.at[index, step - 1, half, side],
            device(lax.rem(t + 8 + way, 8)),
            MESH,
        )

    started = []
    for step in (1, 2, 3, 4):
        for half in (0, 1):
            for index in (0, 1):
                for way in (1, -1):
                    if step > 1 and not (step == 4 and half != (0 if way > 0 else 1)):
                        hop(index, step - 1, half, way).wait_recv()
                    if step == 4 and half != (0 if way > 0 else 1):
                        continue
                    copy = hop(index, step, half, way)
                    copy.start()
                    started.append(copy)
    for index in (0, 1):
        hop(index, 3, 1, 1).wait_recv()
        hop(index, 3, 0, -1).wait_recv()
        hop(index, 4, 0, 1).wait_recv()
        hop(index, 4, 1, -1).wait_recv()
    for copy in started:
        copy.wait_send()
    for index, (ref, _, _) in enumerate(streams):
        part = ref.at[0, pl.ds(0, 31)]
        pltpu.make_async_copy(part, part, send_sem.at[index]).wait()


def spread(vt):
    return pl.pallas_call(
        spread_kernel,
        out_shape=(jax.ShapeDtypeStruct((8, 32, 16, 128), F32),) * 2,
        in_specs=[VMEM],
        out_specs=(VMEM, VMEM),
        scratch_shapes=[
            pltpu.SemaphoreType.DMA((2,)),
            pltpu.SemaphoreType.DMA((2,)),
            pltpu.SemaphoreType.DMA((2,)),
            pltpu.SemaphoreType.DMA((2, 4, 2, 2)),
            pltpu.SemaphoreType.DMA((2, 4, 2, 2)),
        ],
        compiler_params=pltpu.CompilerParams(collective_id=0, has_side_effects=True, vmem_limit_bytes=LIMIT),
        name="spread",
    )(vt)


def stack(x):
    high, low = halves(x)
    return jnp.concatenate([high, low, high, high], axis=0)


def outer_kernel(c0_ref, c1_ref, ga_ref, gb_ref, ea_ref, eb_ref, za_ref, zb_ref):
    y, q, z, act = place()

    def wide_rows(ref, *index):
        return jnp.concatenate([ref[(half,) + index] for half in (0, 1)], axis=-1)

    def own_rows(ref, t):
        return wide_rows(ref, slice(None), pl.ds(t * 8, 8)).reshape(64, 256).astype(BF16)

    mine1 = own_rows(c1_ref, z)
    mine0 = own_rows(c0_ref, y)

    def first_a(w, carry):
        left = ga_ref[:, w, 0:8, :].reshape(64, 128)
        right = ga_ref[:, w, 8:16, :].reshape(64, 128)
        out = jnp.dot(mine1, stack(jnp.concatenate([left, right], axis=1)), preferred_element_type=F32)
        za_ref[:, pl.ds(16 * w, 8), :] = out[:, :128].reshape(8, 8, 128)
        za_ref[:, pl.ds(16 * w + 8, 8), :] = out[:, 128:].reshape(8, 8, 128)
        return carry

    lax.fori_loop(0, 32, first_a, 0, unroll=4)

    def second_a(a, carry):
        left = jnp.concatenate([wide_rows(c0_ref, a, pl.ds(half, 32, stride=2)) for half in (0, 1)], axis=0)
        left = left.astype(BF16)
        for i in range(0, 8, 2):
            right = jnp.concatenate(
                [za_ref[a, pl.ds(i, 64, stride=8), :], za_ref[a, pl.ds(i + 1, 64, stride=8), :]], axis=1
            )
            out = jnp.dot(left, stack(right), preferred_element_type=F32)
            for k in range(2):
                for half in range(2):
                    ea_ref[pl.ds(a * 16 + half * 8 + i + k, 32, stride=128), :] = out[
                        32 * half : 32 * half + 32, 128 * k : 128 * k + 128
                    ]
        return carry

    lax.fori_loop(0, 8, second_a, 0)

    def first_b(s, carry):
        for i in range(0, 8, 2):
            left = gb_ref[:, pl.ds(64 * s + i, 8, stride=8), :].reshape(64, 128)
            right = gb_ref[:, pl.ds(64 * s + i + 1, 8, stride=8), :].reshape(64, 128)
            out = jnp.dot(mine0, stack(jnp.concatenate([left, right], axis=1)), preferred_element_type=F32)
            zb_ref[pl.ds((8 * s + i) * 64, 64), :] = out[:, :128]
            zb_ref[pl.ds((8 * s + i + 1) * 64, 64), :] = out[:, 128:]
        return carry

    lax.fori_loop(0, 8, first_b, 0)

    def second_b(a, carry):
        left = wide_rows(c1_ref, a).astype(BF16)
        for p in range(4):
            right = jnp.concatenate(
                [zb_ref[pl.ds(a * 8 + 2 * p + half, 64, stride=64), :] for half in range(2)], axis=1
            )
            out = jnp.dot(left, stack(right), preferred_element_type=F32)
            for half in range(2):
                eb_ref[:, p, a, pl.ds(half * 8, 8), :] = out[:, 128 * half : 128 * half + 128].reshape(8, 8, 128)
        return carry

    lax.fori_loop(0, 8, second_b, 0)


def outer(c0, c1, ga, gb):
    ea, eb = pl.pallas_call(
        outer_kernel,
        out_shape=(
            jax.ShapeDtypeStruct((4096, 128), F32),
            jax.ShapeDtypeStruct((8, 4, 8, 16, 128), F32),
        ),
        in_specs=[VMEM] * 4,
        out_specs=(VMEM, VMEM),
        scratch_shapes=[pltpu.VMEM((8, 512, 128), F32), pltpu.VMEM((4096, 128), F32)],
        compiler_params=pltpu.CompilerParams(vmem_limit_bytes=LIMIT),
        name="outer",
    )(c0, c1, ga, gb.reshape(8, 512, 128))
    return ea.reshape(32, 2, 64, 128), eb.reshape(8, 4, 2, 64, 128)


def home_kernel(ea_ref, eb_ref, r_ref, send_sem, recv_sem, local_sem):
    y, q, z, act = place()
    wide = 4 * y + q
    row_a = y * 8 + q * 2 + act
    row_b = 64 + z * 8 + q * 2 + act
    barrier = pltpu.get_barrier_semaphore()

    def at_a(step):
        t, p = partner(lax.div(step, 2), y, q)
        g = lax.rem(act + lax.rem(step, 2), 2)
        return ea_ref.at[4 * t + p, g], {"wide": 4 * t + p, "narrow": z, "act": g}

    def at_b(step):
        t, p = partner(lax.div(step, 2), z, q)
        g = lax.rem(act + lax.rem(step, 2), 2)
        return eb_ref.at[t, p, g], {"wide": 4 * y + p, "narrow": t, "act": g}

    def greet(step, carry):
        pl.semaphore_signal(barrier, inc=1, device_id=at_a(step)[1], device_id_type=MESH)
        pl.semaphore_signal(barrier, inc=1, device_id=at_b(step)[1], device_id_type=MESH)
        return carry

    lax.fori_loop(1, 64, greet, 0)
    own = [
        pltpu.make_async_copy(ea_ref.at[wide, act], r_ref.at[row_a], local_sem.at[0]),
        pltpu.make_async_copy(eb_ref.at[z, q, act], r_ref.at[row_b], local_sem.at[1]),
    ]
    for copy in own:
        copy.start()
    pl.semaphore_wait(barrier, 126)

    def send(step, carry):
        src, device = at_a(step)
        pltpu.make_async_remote_copy(
            src, r_ref.at[row_a], send_sem.at[0], recv_sem.at[0], device, MESH
        ).start()
        src, device = at_b(step)
        pltpu.make_async_remote_copy(
            src, r_ref.at[row_b], send_sem.at[1], recv_sem.at[1], device, MESH
        ).start()
        return carry

    lax.fori_loop(1, 64, send, 0)
    for copy in own:
        copy.wait()
    for index in (0, 1):
        part = r_ref.at[pl.ds(0, 63)]
        pltpu.make_async_copy(part, part, recv_sem.at[index]).wait()
        pltpu.make_async_copy(part, part, send_sem.at[index]).wait()


def home(ea, eb):
    return pl.pallas_call(
        home_kernel,
        out_shape=jax.ShapeDtypeStruct((128, 64, 128), F32),
        in_specs=[VMEM, VMEM],
        out_specs=VMEM,
        scratch_shapes=[pltpu.SemaphoreType.DMA((2,))] * 3,
        compiler_params=pltpu.CompilerParams(collective_id=1, has_side_effects=True, vmem_limit_bytes=LIMIT),
        name="home",
    )(ea, eb)


def inner_kernel(u_ref, third_ref, fourth_ref, w2_ref, w3_ref, r_ref, score_ref, lse_ref):
    def one(j, carry):
        scores = []
        for a in range(4):
            rows = r_ref[pl.ds(a * 16 + j, 128, stride=64), :]
            high, low = halves(rows)
            mid = jnp.dot(
                w2_ref[a], jnp.concatenate([high, low, high], axis=0), preferred_element_type=F32
            )
            high, low = halves(mid)
            expected = lax.dot_general(
                jnp.concatenate([high, low, high], axis=1),
                w3_ref[a],
                (((1,), (1,)), ((), ())),
                preferred_element_type=F32,
            )
            util = (u_ref[a, j] + third_ref[:, a : a + 1]) + fourth_ref[a : a + 1, :]
            score = util + DISCOUNT * expected
            score_ref[a, j] = score
            scores.append(score)
        top = jnp.maximum(jnp.maximum(scores[0], scores[1]), jnp.maximum(scores[2], scores[3]))
        total = sum(jnp.exp(s - top) for s in scores)
        lse_ref[j] = top + jnp.log(total)
        return carry

    lax.fori_loop(0, 16, one, 0)


def inner(u, third, fourth, w2, w3, r):
    return pl.pallas_call(
        inner_kernel,
        out_shape=(
            jax.ShapeDtypeStruct((4, 16, 128, 128), F32),
            jax.ShapeDtypeStruct((16, 128, 128), F32),
        ),
        in_specs=[SMEM] + [VMEM] * 5,
        out_specs=(VMEM, VMEM),
        compiler_params=pltpu.CompilerParams(vmem_limit_bytes=LIMIT),
        name="inner",
    )(u, third, fourth, w2, w3, r.reshape(8192, 128))


def body(
    value_now,
    cost_first,
    cost_second,
    cost_third,
    cost_fourth,
    trans_weights,
    trans_offsets,
    action_order,
):
    act = lax.axis_index("act")
    mine = lax.dynamic_slice_in_dim(action_order, act * 4, 4)
    start_first = lax.axis_index("wide") * 2
    start_second = lax.axis_index("narrow") * 8
    util_first = lax.dynamic_slice_in_dim(jnp.take(cost_first, mine, axis=0), start_first, 2, 1)
    util_second = lax.dynamic_slice_in_dim(jnp.take(cost_second, mine, axis=0), start_second, 8, 1)
    u = (util_first[:, :, None] + util_second[:, None, :]).reshape(4, 16)
    third = jnp.take(cost_third, mine, axis=0).T
    fourth = jnp.take(cost_fourth, mine, axis=0)

    c0, c1, w2, w3 = build(action_order, trans_offsets, trans_weights)
    vt = value_now.transpose(2, 0, 1, 3).reshape(128, 16, 128)
    ga, gb = spread(vt)
    ea, eb = outer(c0, c1, ga, gb)
    r = home(ea, eb)
    scores, lse = inner(u, third, fourth, w2, w3, r)
    other = lax.ppermute(lse, "act", [(0, 1), (1, 0)])
    top = jnp.maximum(lse, other)
    new_value = top + jnp.log(jnp.exp(lse - top) + jnp.exp(other - top))
    choice_prob = jnp.exp(scores - new_value).astype(BF16)
    return new_value.reshape(2, 8, 128, 128), choice_prob.reshape(4, 2, 8, 128, 128)


def solution(mesh):
    return jax.shard_map(
        body,
        mesh=mesh,
        in_specs=(P("wide", "narrow", None, None), P(), P(), P(), P(), P(), P(), P()),
        out_specs=(P("wide", "narrow", None, None), P("act", "wide", "narrow", None, None)),
        check_vma=False,
    )
```

time: 511 us -> 211 us (0.41); the launches traced: 501 us -> 211 us
  waiting for transfers between devices: 243 us -> 24.9 us
  Pallas kernels: 0 us -> 164 us
  blocking collectives: 96.6 us -> 0 us
  matrix products: 55 us -> 0 us
  starting transfers between devices: 31.8 us -> 2.09 us
  local copies, waits for them, and re-layouts: 33.2 us -> 11.3 us
  other arithmetic: 26.3 us -> 7.73 us
  between operations: 14.8 us -> 0.7 us
    all_to_all x3 -> x0, waiting for transfers between devices: 166 us -> none  [the longest x1 86.7 us: body(): lax.all_to_all(field, 'wide', split_axis=3, concat_axis=1, tiled=True)]
    pallas_call x0 -> x5, Pallas kernels: none -> 164 us  [the longest x1 67.4 us: home(): pl.pallas_call(home_kernel, out_shape=jax.ShapeDtypeStruct((128, 64, 128)...]
    all_to_all x1 -> x0, blocking collectives: 96.6 us -> none  [body(): lax.all_to_all(field, 'narrow', split_axis=2, concat_axis=3, tiled=True)]
    all_gather x2 -> x0, waiting for transfers between devices: 77.5 us -> none  [merged(): pieces = jax.tree.map(lambda part: lax.all_gather(part, axis), value)]
    dot_general x8 -> x0, matrix products: 55 us -> none  [the longest x4 32.7 us: transition(): return jnp.einsum('ijk,j->ik', matched, normed, precision=HIGHEST)]
    all_to_all x3 -> x0, starting transfers between devices: 31.7 us -> none  [the longest x1 13.2 us: body(): lax.all_to_all(field, 'wide', split_axis=3, concat_axis=1, tiled=True)]
    ppermute x0 -> x1, waiting for transfers between devices: none -> 24.9 us  [body(): other = lax.ppermute(lse, 'act', [(0, 1), (1, 0)])]
    eq x2 -> x0, other arithmetic: 13.6 us -> none  [transition(): target[:, :, None] == row_ids[None, None, :]]
  transfers between devices with their start and end apart: 5 -> 1, of which waited for: 5 -> 1; matrix products, arithmetic and copies ran while one was open for 11% -> 0% of each run, Pallas kernels for 0% -> 0%
where the time goes in v1:
time: 211 us
  Pallas kernels  164 us (78%)
  waiting for transfers between devices  24.9 us (12%)
  local copies, waits for them, and re-layouts  11.3 us (5%)
  other arithmetic  7.73 us (4%)
    pallas_call x1, Pallas kernels, home(): pl.pallas_call(home_kernel, out_shape=jax.ShapeDtypeStruct((128, 64, 128)...  67.4 us
    pallas_call x1, Pallas kernels, spread(): pl.pallas_call(spread_kernel, out_shape=(jax.ShapeDtypeStruct((8, 32, 16,...  52.1 us
    ppermute x1, waiting for transfers between devices, body(): other = lax.ppermute(lse, 'act', [(0, 1), (1, 0)])  24.9 us
    pallas_call x1, Pallas kernels, inner(): pl.pallas_call(inner_kernel, out_shape=(jax.ShapeDtypeStruct((4, 16, 128,...  19.7 us
    pallas_call x1, Pallas kernels, outer(): pl.pallas_call(outer_kernel, out_shape=(jax.ShapeDtypeStruct((4096, 128),...  12.9 us
    pallas_call x1, Pallas kernels, build(): pl.pallas_call(build_kernel, out_shape=(jax.ShapeDtypeStruct((2, 8, 64, 1...  12.1 us
    convert_element_type x1, other arithmetic, body(): choice_prob = jnp.exp(scores - new_value).astype(BF16)  4.53 us
  transfers between devices with their start and end apart: 1, of which 1 were waited for; matrix products, arithmetic and copies ran while one was open for 0% of the time, Pallas kernels for 0%

profile of v1, /device:TPU:1, one launch (start us, length us, event | category | flops | bytes accessed | tf_op | source)
XLA Modules:
  0.0 210.9 jit_solution(1777692959152251439)
XLA Ops:
  0.6 0.0 copy-start
  0.7 0.7 compare_and_fusion
  1.4 0.0 copy-done
  1.4 0.6 gather_fusion.3
  2.0 1.2 gather_fusion.2
  3.2 1.2 gather_fusion.1
  4.5 1.2 gather_fusion
  5.7 0.1 broadcast_select_fusion.3
  5.8 0.1 constant_dynamic-slice_fusion.1
  5.9 0.1 constant_dynamic-slice_fusion
  5.9 0.1 broadcast_add_fusion
  6.0 0.7 add.46.u_ref
  6.7 1.4 copy.16.offs_ref
  8.0 0.7 broadcast_select_fusion
  8.7 0.7 copy.15
  9.4 2.8 %copy.19 = f32[128,2,8,128]{3,2,1,0:T(8,128)} copy(f32[128,2,8,128]{3,0,2,1:T(8,128)} %bitcast.18) | data formatting | bytes 2097152 | tf_op jit(solution)/shard_map/transpose | solution.py:409
  12.2 52.1 %spread.1 = (f32[8,32,16,128]{3,2,1,0:T(8,128)}, f32[8,32,16,128]{3,2,1,0:T(8,128)}) custom-call(f32[128,16,128]{2,1,0:T(8,128)} %bitcast.13), custom_call_target="tpu_custom_call" | custom-call | tf_op jit(solution)/shard_map/spread/pallas_call | solution.py:181
  64.3 1.3 pad.4.w_ref
  65.7 12.1 %build.1 = (f32[2,8,64,128]{3,2,1,0:T(8,128)}, f32[2,8,64,128]{3,2,1,0:T(8,128)}, bf16[4,128,384]{2,1,0:T(8,128)(2,1)}, bf16[4,128,384]{2,1,0:T(8,128)(2,1)}) custom-call(s32[8]{0:T(128)} %order_ref.1, s32[8,4]{1,0:T(8,128)} %copy.16.offs_ref, f32[8,4,256]{2,1,0:T(4,128)} %pad.4.w_ref), custom_call_target="tpu_custom_call" | custom-call | tf_op jit(solution)/shard_map/build/pallas_call | solution.py:79
  77.7 12.9 %outer.1 = (f32[4096,128]{1,0:T(8,128)}, f32[8,4,8,16,128]{4,3,2,1,0:T(8,128)}) custom-call(f32[2,8,64,128]{3,2,1,0:T(8,128)} %get-tuple-element.16.c0_ref, f32[2,8,64,128]{3,2,1,0:T(8,128)} %get-tuple-element.17.c1_ref, f32[8,32,16,128]{3,2,1,0:T(8,128)} %get-tuple-element.18.ga_ref, f32[8,512,128]{2,1,0:T(8,128)} %bitcast.15), custom_call_target="tpu_custom_call" | custom-call | tf_op jit(solution)/shard_map/outer/pallas_call | solution.py:268
  90.6 67.4 %home.1 = f32[128,64,128]{2,1,0:T(8,128)} custom-call(f32[32,2,64,128]{3,2,1,0:T(8,128)} %bitcast.16, f32[8,4,2,64,128]{4,3,2,1,0:T(8,128)} %bitcast.17), custom_call_target="tpu_custom_call" | custom-call | tf_op jit(solution)/shard_map/home/pallas_call | solution.py:335
  157.9 19.7 %inner.1 = (f32[4,16,128,128]{3,2,1,0:T(8,128)}, f32[16,128,128]{2,1,0:T(8,128)}) custom-call(f32[4,16]{1,0:T(4,128)} %add.46.u_ref, f32[128,4]{1,0:T(8,128)} %bitcast.19, f32[4,128]{1,0:T(4,128)} %get-tuple-element.26.fourth_ref, bf16[4,128,384]{2,1,0:T(8,128)(2,1)} %get-tuple-element.14.w2_ref, bf16[4,128,384]{2,1,0:T(8,128)(2,1)} %get-tuple-element.15.w3_ref, ...), custom_call_target="tpu_custom_call" | custom-call | tf_op jit(solution)/shard_map/inner/pallas_call | solution.py:375
  177.6 2.1 collective-permute-start
  179.8 24.9 %collective-permute-done = f32[16,128,128]{2,1,0:T(8,128)S(1)} collective-permute-done((f32[16,128,128]{2,1,0:T(8,128)}, f32[16,128,128]{2,1,0:T(8,128)S(1)}, u32[]{:S(2)}, u32[]{:S(2)}) %collective-permute-start) | collective-permute-done | bytes 1048608 | tf_op jit(solution)/shard_map/ppermute | solution.py:414
  204.7 1.6 log_add_fusion
  206.3 0.0 copy-start.1
  206.3 4.5 %exponential_convert_fusion = bf16[4,16,128,128]{3,2,1,0:T(8,128)(2,1)} fusion(f32[4,16,128,128]{3,2,1,0:T(8,128)} %get-tuple-element.23, f32[16,128,128]{2,1,0:T(8,128)S(1)} %log_add_fusion), kind=kLoop, calls=%fused_computation.4 | loop fusion | flops 2097152 | bytes 7340032 | tf_op jit(solution)/shard_map/convert_element_type | solution.py:417
  210.9 0.0 copy-done.1
  (1 shorter events, 0.0 us)
Async XLA Ops:
  0.6 0.8 copy-start
  177.6 27.0 %collective-permute-start = (f32[16,128,128]{2,1,0:T(8,128)}, f32[16,128,128]{2,1,0:T(8,128)S(1)}, u32[]{:S(2)}, u32[]{:S(2)}) collective-permute-start(f32[16,128,128]{2,1,0:T(8,128)} %get-tuple-element.22), channel_id=1, source_target_pairs={{0,1},{1,0},{2,3},{3,2},{4,5},{5,4},{6,7},{7,6},{8,9},{9,8},{10,11... | collective-permute-start | bytes 3145736 | tf_op jit(solution)/shard_map/ppermute | solution.py:414
  206.3 4.5 %copy-start.1 = (f32[16,128,128]{2,1,0:T(8,128)}, f32[16,128,128]{2,1,0:T(8,128)S(1)}, u32[]{:S(2)}) copy-start(f32[16,128,128]{2,1,0:T(8,128)S(1)} %log_add_fusion) | copy-start | bytes 3145732

commit v2 on v1

--- a/solution.py
+++ b/solution.py
@@ -29,19 +29,26 @@
     return high, low
 
 
-def build_kernel(order_ref, offs_ref, w_ref, c0_ref, c1_ref, w2_ref, w3_ref):
+def build_kernel(
+    order_ref, offs_ref, first_ref, second_ref, w_ref, third_ref, fourth_ref,
+    c0_ref, c1_ref, w2_ref, w3_ref, u_ref, column_ref, row_ref, pad_ref,
+):
     act = lax.axis_index("act")
+    first_row = lax.axis_index("wide") * 2
+    second_row = lax.axis_index("narrow") * 8
+    pad_ref[...] = jnp.zeros_like(pad_ref)
+    pad_ref[:, :, 0:65] = w_ref[...]
 
     def toeplitz(a, d, length):
-        row = w_ref[pl.ds(a, 1), d, :]
+        row = pad_ref[pl.ds(a, 1), d, :]
         row = row / jnp.sum(row)
-        shift = lax.rem(offs_ref[a, d] - 32 + 256, 256)
+        shift = lax.rem(offs_ref[d, a] - 32 + 256, 256)
         spread = jnp.broadcast_to(pltpu.roll(jnp.broadcast_to(row, (8, 256)), shift, 1)[0:1], (length, 256))
         number = lax.broadcasted_iota(jnp.int32, (length, 256), 0)
         lane = lax.broadcasted_iota(jnp.int32, (length, 256), 1)
         bit = 1
         while bit < length:
-            spread = jnp.where(lax.rem(lax.div(number, bit), 2) == 1, pltpu.roll(spread, bit, 1), spread)
+            spread = jnp.where((number & bit) != 0, pltpu.roll(spread, bit, 1), spread)
             bit *= 2
         zero = jnp.zeros_like(spread)
         below = jnp.sum(jnp.where(lane >= 192, spread, zero), axis=1, keepdims=True)
@@ -69,13 +76,16 @@
             ref[j, :, 0:128] = high[:, :128].astype(BF16)
             ref[j, :, 128:256] = high[:, :128].astype(BF16)
             ref[j, :, 256:384] = low[:, :128].astype(BF16)
+        column_ref[j] = jnp.broadcast_to(third_ref[pl.ds(a, 1), :], (128, 128)).T
+        row_ref[j] = jnp.broadcast_to(fourth_ref[pl.ds(a, 1), :], (8, 128))
+        for k in range(16):
+            u_ref[j, k] = first_ref[a, first_row + k // 8] + second_ref[a, second_row + k % 8]
         return carry
 
     lax.fori_loop(0, 4, mine, 0)
 
 
-def build(order, offsets, weights):
-    padded = jnp.pad(weights, ((0, 0), (0, 0), (0, 256 - weights.shape[2])))
+def build(order, offsets, weights, first, second, third, fourth):
     return pl.pallas_call(
         build_kernel,
         out_shape=(
@@ -83,11 +93,15 @@
             jax.ShapeDtypeStruct((2, 8, 64, 128), F32),
             jax.ShapeDtypeStruct((4, 128, 384), BF16),
             jax.ShapeDtypeStruct((4, 128, 384), BF16),
+            jax.ShapeDtypeStruct((4, 16), F32),
+            jax.ShapeDtypeStruct((4, 128, 128), F32),
+            jax.ShapeDtypeStruct((4, 8, 128), F32),
         ),
-        in_specs=[SMEM, SMEM, VMEM],
-        out_specs=(VMEM,) * 4,
+        in_specs=[SMEM] * 4 + [VMEM] * 3,
+        out_specs=(VMEM, VMEM, VMEM, VMEM, SMEM, VMEM, VMEM),
+        scratch_shapes=[pltpu.VMEM((8, 4, 256), F32)],
         name="build",
-    )(order, offsets, padded)
+    )(order, offsets.T, first, second, weights, third, fourth)
 
 
 def spread_kernel(vt_ref, ga_ref, gb_ref, send_sem, recv_sem, local_sem, ring_send, ring_recv):
@@ -232,7 +246,8 @@
             out = jnp.dot(left, stack(right), preferred_element_type=F32)
             for k in range(2):
                 for half in range(2):
-                    ea_ref[pl.ds(a * 16 + half * 8 + i + k, 32, stride=128), :] = out[
+                    start = lax.div(a, 4) * 64 + half * 32 + (i + k) // 4 * 16 + lax.rem(a, 4) * 4 + (i + k) % 4
+                    ea_ref[pl.ds(start, 32, stride=128), :] = out[
                         32 * half : 32 * half + 32, 128 * k : 128 * k + 128
                     ]
         return carry
@@ -250,18 +265,20 @@
 
     lax.fori_loop(0, 8, first_b, 0)
 
-    def second_b(a, carry):
-        left = wide_rows(c1_ref, a).astype(BF16)
-        for p in range(4):
-            right = jnp.concatenate(
-                [zb_ref[pl.ds(a * 8 + 2 * p + half, 64, stride=64), :] for half in range(2)], axis=1
-            )
-            out = jnp.dot(left, stack(right), preferred_element_type=F32)
-            for half in range(2):
-                eb_ref[:, p, a, pl.ds(half * 8, 8), :] = out[:, 128 * half : 128 * half + 128].reshape(8, 8, 128)
-        return carry
-
-    lax.fori_loop(0, 8, second_b, 0)
+    def second_b(g, carry):
+        for a in range(4):
+            left = wide_rows(c1_ref, 4 * g + a).astype(BF16)
+            for p in range(4):
+                start = (4 * g + a) * 8 + 2 * p
+                right = jnp.concatenate([zb_ref[pl.ds(start + k, 64, stride=64), :] for k in range(2)], axis=1)
+                out = jnp.dot(left, stack(right), preferred_element_type=F32)
+                for k in range(2):
+                    block = out[:, 128 * k : 128 * k + 128].reshape(8, 8, 128)
+                    for half in range(2):
+                        eb_ref[:, p, g, 2 * k + half, 4 * a : 4 * a + 4, :] = block[:, 4 * half : 4 * half + 4]
+        return carry
+
+    lax.fori_loop(0, 2, second_b, 0)
 
 
 def outer(c0, c1, ga, gb):
@@ -269,7 +286,7 @@
         outer_kernel,
         out_shape=(
             jax.ShapeDtypeStruct((4096, 128), F32),
-            jax.ShapeDtypeStruct((8, 4, 8, 16, 128), F32),
+            jax.ShapeDtypeStruct((8, 4, 2, 4, 16, 128), F32),
         ),
         in_specs=[VMEM] * 4,
         out_specs=(VMEM, VMEM),
@@ -277,10 +294,14 @@
         compiler_params=pltpu.CompilerParams(vmem_limit_bytes=LIMIT),
         name="outer",
     )(c0, c1, ga, gb.reshape(8, 512, 128))
-    return ea.reshape(32, 2, 64, 128), eb.reshape(8, 4, 2, 64, 128)
-
-
-def home_kernel(ea_ref, eb_ref, r_ref, send_sem, recv_sem, local_sem):
+    return ea.reshape(32, 2, 4, 16, 128), eb
+
+
+def home_kernel(
+    u_ref, column_ref, row_ref, w2_ref, w3_ref, ea_ref, eb_ref,
+    value_ref, prob_ref,
+    r_ref, score_ref, lse_ref, other_ref, send_sem, recv_sem, local_sem, lse_send, lse_recv,
+):
     y, q, z, act = place()
     wide = 4 * y + q
     row_a = y * 8 + q * 2 + act
@@ -303,86 +324,127 @@
         return carry
 
     lax.fori_loop(1, 64, greet, 0)
-    own = [
-        pltpu.make_async_copy(ea_ref.at[wide, act], r_ref.at[row_a], local_sem.at[0]),
-        pltpu.make_async_copy(eb_ref.at[z, q, act], r_ref.at[row_b], local_sem.at[1]),
-    ]
+    own = []
+    for c in range(4):
+        own += [
+            pltpu.make_async_copy(ea_ref.at[wide, act, c], r_ref.at[c, row_a], local_sem.at[0, c]),
+            pltpu.make_async_copy(eb_ref.at[z, q, act, c], r_ref.at[c, row_b], local_sem.at[1, c]),
+        ]
     for copy in own:
         copy.start()
     pl.semaphore_wait(barrier, 126)
 
-    def send(step, carry):
-        src, device = at_a(step)
-        pltpu.make_async_remote_copy(
-            src, r_ref.at[row_a], send_sem.at[0], recv_sem.at[0], device, MESH
-        ).start()
-        src, device = at_b(step)
-        pltpu.make_async_remote_copy(
-            src, r_ref.at[row_b], send_sem.at[1], recv_sem.at[1], device, MESH
-        ).start()
-        return carry
-
-    lax.fori_loop(1, 64, send, 0)
+    def send_chunk(c):
+        def send(step, carry):
+            src, device = at_a(step)
+            pltpu.make_async_remote_copy(
+                src.at[c], r_ref.at[c, row_a], send_sem.at[0, c], recv_sem.at[0, c], device, MESH
+            ).start()
+            src, device = at_b(step)
+            pltpu.make_async_remote_copy(
+                src.at[c], r_ref.at[c, row_b], send_sem.at[1, c], recv_sem.at[1, c], device, MESH
+            ).start()
+            return carry
+
+        lax.fori_loop(1, 64, send, 0)
+
+    def settle(c, sem):
+        for index in (0, 1):
+            part = r_ref.at[c, pl.ds(0, 63)]
+            pltpu.make_async_copy(part, part, sem.at[index, c]).wait()
+
+    def swap(c):
+        return pltpu.make_async_remote_copy(
+            lse_ref.at[c], other_ref.at[c], lse_send.at[c], lse_recv.at[c], {"act": 1 - act}, MESH
+        )
+
+    def compute(c):
+        flat = r_ref.at[c].reshape(2048, 128)
+        for a in range(4):
+            for j in (0, 2):
+                rows = jnp.concatenate(
+                    [flat[pl.ds(4 * a + j + k, 128, stride=16), :] for k in range(2)], axis=1
+                )
+                high, low = halves(rows)
+                mid = jnp.dot(w2_ref[a], jnp.concatenate([high, low, high], axis=0), preferred_element_type=F32)
+                high, low = halves(jnp.concatenate([mid[:, :128], mid[:, 128:]], axis=0))
+                expected = lax.dot_general(
+                    jnp.concatenate([high, low, high], axis=1),
+                    w3_ref[a],
+                    (((1,), (1,)), ((), ())),
+                    preferred_element_type=F32,
+                )
+                for k in range(2):
+                    util = (u_ref[a, 4 * c + j + k] + column_ref[a]) + row_ref[a, 0:1, :]
+                    score_ref[a, 4 * c + j + k] = util + DISCOUNT * expected[128 * k : 128 * k + 128]
+
+        def total(j, carry):
+            scores = [score_ref[a, 4 * c + j] for a in range(4)]
+            top = jnp.maximum(jnp.maximum(scores[0], scores[1]), jnp.maximum(scores[2], scores[3]))
+            summed = sum(jnp.exp(s - top) for s in scores)
+            lse_ref[c, j] = top + jnp.log(summed)
+            return carry
+
+        lax.fori_loop(0, 4, total, 0)
+
+    def finish(c):
+        swap(c).wait_recv()
+
+        def one(j, carry):
+            ours, theirs = lse_ref[c, j], other_ref[c, j]
+            top = jnp.maximum(ours, theirs)
+            value = top + jnp.log(jnp.exp(ours - top) + jnp.exp(theirs - top))
+            value_ref[4 * c + j] = value
+            for a in range(4):
+                prob_ref[a, 4 * c + j] = jnp.exp(score_ref[a, 4 * c + j] - value).astype(BF16)
+            return carry
+
+        lax.fori_loop(0, 4, one, 0)
+
+    send_chunk(0)
+    send_chunk(1)
     for copy in own:
         copy.wait()
-    for index in (0, 1):
-        part = r_ref.at[pl.ds(0, 63)]
-        pltpu.make_async_copy(part, part, recv_sem.at[index]).wait()
-        pltpu.make_async_copy(part, part, send_sem.at[index]).wait()
-
-
-def home(ea, eb):
+    for c in range(4):
+        settle(c, recv_sem)
+        if c < 2:
+            send_chunk(c + 2)
+        if c > 0:
+            swap(c - 1).start()
+        compute(c)
+        if c > 0:
+            finish(c - 1)
+    swap(3).start()
+    for c in range(4):
+        settle(c, send_sem)
+    finish(3)
+    for c in range(4):
+        swap(c).wait_send()
+
+
+def home(u, column, row, w2, w3, ea, eb):
     return pl.pallas_call(
         home_kernel,
-        out_shape=jax.ShapeDtypeStruct((128, 64, 128), F32),
-        in_specs=[VMEM, VMEM],
-        out_specs=VMEM,
-        scratch_shapes=[pltpu.SemaphoreType.DMA((2,))] * 3,
+        out_shape=(
+            jax.ShapeDtypeStruct((16, 128, 128), F32),
+            jax.ShapeDtypeStruct((4, 16, 128, 128), BF16),
+        ),
+        in_specs=[SMEM] + [VMEM] * 6,
+        out_specs=(VMEM, VMEM),
+        scratch_shapes=[
+            pltpu.VMEM((4, 128, 16, 128), F32),
+            pltpu.VMEM((4, 16, 128, 128), F32),
+            pltpu.VMEM((4, 4, 128, 128), F32),
+            pltpu.VMEM((4, 4, 128, 128), F32),
+            pltpu.SemaphoreType.DMA((2, 4)),
+            pltpu.SemaphoreType.DMA((2, 4)),
+            pltpu.SemaphoreType.DMA((2, 4)),
+            pltpu.SemaphoreType.DMA((4,)),
+            pltpu.SemaphoreType.DMA((4,)),
+        ],
         compiler_params=pltpu.CompilerParams(collective_id=1, has_side_effects=True, vmem_limit_bytes=LIMIT),
         name="home",
-    )(ea, eb)
-
-
-def inner_kernel(u_ref, third_ref, fourth_ref, w2_ref, w3_ref, r_ref, score_ref, lse_ref):
-    def one(j, carry):
-        scores = []
-        for a in range(4):
-            rows = r_ref[pl.ds(a * 16 + j, 128, stride=64), :]
-            high, low = halves(rows)
-            mid = jnp.dot(
-                w2_ref[a], jnp.concatenate([high, low, high], axis=0), preferred_element_type=F32
-            )
-            high, low = halves(mid)
-            expected = lax.dot_general(
-                jnp.concatenate([high, low, high], axis=1),
-                w3_ref[a],
-                (((1,), (1,)), ((), ())),
-                preferred_element_type=F32,
-            )
-            util = (u_ref[a, j] + third_ref[:, a : a + 1]) + fourth_ref[a : a + 1, :]
-            score = util + DISCOUNT * expected
-            score_ref[a, j] = score
-            scores.append(score)
-        top = jnp.maximum(jnp.maximum(scores[0], scores[1]), jnp.maximum(scores[2], scores[3]))
-        total = sum(jnp.exp(s - top) for s in scores)
-        lse_ref[j] = top + jnp.log(total)
-        return carry
-
-    lax.fori_loop(0, 16, one, 0)
-
-
-def inner(u, third, fourth, w2, w3, r):
-    return pl.pallas_call(
-        inner_kernel,
-        out_shape=(
-            jax.ShapeDtypeStruct((4, 16, 128, 128), F32),
-            jax.ShapeDtypeStruct((16, 128, 128), F32),
-        ),
-        in_specs=[SMEM] + [VMEM] * 5,
-        out_specs=(VMEM, VMEM),
-        compiler_params=pltpu.CompilerParams(vmem_limit_bytes=LIMIT),
-        name="inner",
-    )(u, third, fourth, w2, w3, r.reshape(8192, 128))
+    )(u, column, row, w2, w3, ea, eb)
 
 
 def body(
@@ -395,26 +457,13 @@
     trans_offsets,
     action_order,
 ):
-    act = lax.axis_index("act")
-    mine = lax.dynamic_slice_in_dim(action_order, act * 4, 4)
-    start_first = lax.axis_index("wide") * 2
-    start_second = lax.axis_index("narrow") * 8
-    util_first = lax.dynamic_slice_in_dim(jnp.take(cost_first, mine, axis=0), start_first, 2, 1)
-    util_second = lax.dynamic_slice_in_dim(jnp.take(cost_second, mine, axis=0), start_second, 8, 1)
-    u = (util_first[:, :, None] + util_second[:, None, :]).reshape(4, 16)
-    third = jnp.take(cost_third, mine, axis=0).T
-    fourth = jnp.take(cost_fourth, mine, axis=0)
-
-    c0, c1, w2, w3 = build(action_order, trans_offsets, trans_weights)
+    c0, c1, w2, w3, u, column, row = build(
+        action_order, trans_offsets, trans_weights, cost_first, cost_second, cost_third, cost_fourth
+    )
     vt = value_now.transpose(2, 0, 1, 3).reshape(128, 16, 128)
     ga, gb = spread(vt)
     ea, eb = outer(c0, c1, ga, gb)
-    r = home(ea, eb)
-    scores, lse = inner(u, third, fourth, w2, w3, r)
-    other = lax.ppermute(lse, "act", [(0, 1), (1, 0)])
-    top = jnp.maximum(lse, other)
-    new_value = top + jnp.log(jnp.exp(lse - top) + jnp.exp(other - top))
-    choice_prob = jnp.exp(scores - new_value).astype(BF16)
+    new_value, choice_prob = home(u, column, row, w2, w3, ea, eb)
     return new_value.reshape(2, 8, 128, 128), choice_prob.reshape(4, 2, 8, 128, 128)
 
 

time: 211 us -> 173 us (0.82)
  waiting for transfers between devices: 24.9 us -> 0 us
  other arithmetic: 7.73 us -> 0 us
  local copies, waits for them, and re-layouts: 11.3 us -> 6.57 us
    ppermute x1 -> x0, waiting for transfers between devices: 24.9 us -> none  [body(): other = lax.ppermute(lse, 'act', [(0, 1), (1, 0)])]
    convert_element_type x1 -> x0, other arithmetic: 4.53 us -> none  [body(): choice_prob = jnp.exp(scores - new_value).astype(BF16)]
    gather x4 -> x0, local copies, waits for them, and re-layouts: 4.3 us -> none  [the longest x1 1.25 us: body(): third = jnp.take(cost_third, mine, axis=0).T]
    unnamed x5 -> x4, local copies, waits for them, and re-layouts: 1.37 us -> 3.77 us
    pallas_call x2 -> x1, Pallas kernels: 87.1 us -> 88.5 us  [home(): pl.pallas_call(home_kernel, out_shape=(jax.ShapeDtypeStruct((16, 128, 128...]
  transfers between devices with their start and end apart: 1 -> 0, of which waited for: 1 -> 0; matrix products, arithmetic and copies ran while one was open for 0% -> 0% of each run, Pallas kernels for 0% -> 0%
where the time goes in v2:
time: 173 us; the launch traced here: 172 us
  Pallas kernels  165 us (95%)
  local copies, waits for them, and re-layouts  6.57 us (4%)
    pallas_call x1, Pallas kernels, home(): pl.pallas_call(home_kernel, out_shape=(jax.ShapeDtypeStruct((16, 128, 128...  88.5 us
    pallas_call x1, Pallas kernels, spread(): pl.pallas_call(spread_kernel, out_shape=(jax.ShapeDtypeStruct((8, 32, 16,...  52.2 us
    pallas_call x1, Pallas kernels, build(): pl.pallas_call(build_kernel, out_shape=(jax.ShapeDtypeStruct((2, 8, 64, 1...  12.8 us
    pallas_call x1, Pallas kernels, outer(): pl.pallas_call(outer_kernel, out_shape=(jax.ShapeDtypeStruct((4096, 128),...  11.6 us
    unnamed x4, local copies, waits for them, and re-layouts  3.77 us

profile of v2, /device:TPU:1, one launch (start us, length us, event | category | flops | bytes accessed | tf_op | source)
XLA Modules:
  0.0 172.3 jit_solution(438676124791336842)
XLA Ops:
  0.6 2.8 %copy.12 = f32[128,2,8,128]{3,2,1,0:T(8,128)} copy(f32[128,2,8,128]{3,0,2,1:T(8,128)} %bitcast.13) | data formatting | bytes 2097152 | tf_op jit(solution)/shard_map/transpose | solution.py:463
  3.4 12.8 %build.1 = (f32[2,8,64,128]{3,2,1,0:T(8,128)}, f32[2,8,64,128]{3,2,1,0:T(8,128)}, bf16[4,128,384]{2,1,0:T(8,128)(2,1)}, bf16[4,128,384]{2,1,0:T(8,128)(2,1)}, f3...) custom-call(s32[8]{0:T(128)} %order_ref.1, s32[4,8]{1,0:T(4,128)} %bitcast.15, f32[8,64]{1,0:T(8,128)} %first_ref.1, ...), custom_call_target="tpu_custom_call" | custom-call | tf_op jit(solution)/shard_map/build/pallas_call | solution.py:89
  16.2 52.2 %spread.1 = (f32[8,32,16,128]{3,2,1,0:T(8,128)}, f32[8,32,16,128]{3,2,1,0:T(8,128)}) custom-call(f32[128,16,128]{2,1,0:T(8,128)} %bitcast.9), custom_call_target="tpu_custom_call" | custom-call | tf_op jit(solution)/shard_map/spread/pallas_call | solution.py:195
  68.4 11.6 %outer.1 = (f32[4096,128]{1,0:T(8,128)}, f32[8,4,2,4,16,128]{5,4,3,2,1,0:T(8,128)}) custom-call(f32[2,8,64,128]{3,2,1,0:T(8,128)} %get-tuple-element.20.c0_ref, f32[2,8,64,128]{3,2,1,0:T(8,128)} %get-tuple-element.21.c1_ref, f32[8,32,16,128]{3,2,1,0:T(8,128)} %get-tuple-element.22.ga_ref, f32[8,512,128]{2,1,0:T(8,128)} %bitcast.12), custom_call_target="tpu_custom_call" | custom-call | tf_op jit(solution)/shard_map/outer/pallas_call | solution.py:285
  80.1 88.5 %home.1 = (f32[16,128,128]{2,1,0:T(8,128)}, bf16[4,16,128,128]{3,2,1,0:T(8,128)(2,1)}) custom-call(f32[4,16]{1,0:T(4,128)} %get-tuple-element.15.u_ref, f32[4,128,128]{2,1,0:T(8,128)} %get-tuple-element.16.column_ref, f32[4,8,128]{2,1,0:T(8,128)} %get-tuple-element.17.row_ref, bf16[4,128,384]{2,1,0:T(8,128)(2,1)} %get-tuple-element.18.w2_ref, ...), custom_call_target="tpu_custom_call" | custom-call | tf_op jit(solution)/shard_map/home/pallas_call | solution.py:426
  168.6 0.0 copy-start
  168.6 2.4 %copy.15 = f32[2,8,128,128]{3,2,1,0:T(8,128)} copy(f32[2,8,128,128]{3,2,1,0:T(8,128)} %bitcast.14) | data formatting | bytes 2097152
  171.0 0.0 copy-done
  171.0 1.3 copy.16
Async XLA Ops:
  168.6 2.5 %copy-start = (bf16[4,16,128,128]{3,2,1,0:T(8,128)(2,1)S(1)}, bf16[4,16,128,128]{3,2,1,0:T(8,128)(2,1)}, u32[]{:S(2)}) copy-start(bf16[4,16,128,128]{3,2,1,0:T(8,128)(2,1)} %get-tuple-element.27) | copy-start | bytes 6291460

commit v3 on v0

v3 whole, which is shorter than its diff:
```python
import jax
import jax.numpy as jnp
from jax import lax
from jax.experimental import pallas as pl
from jax.experimental.pallas import tpu as pltpu
from jax.sharding import PartitionSpec as P

DISCOUNT = 0.95
MESH = pl.DeviceIdType.MESH
F32 = jnp.float32
BF16 = jnp.bfloat16
VMEM = pl.BlockSpec(memory_space=pltpu.VMEM)
SMEM = pl.BlockSpec(memory_space=pltpu.SMEM)
LIMIT = 34 * 1024 * 1024


def place():
    wide = lax.axis_index("wide")
    return lax.div(wide, 4), lax.rem(wide, 4), lax.axis_index("narrow"), lax.axis_index("act")


def partner(step, t, q, sign):
    near = lax.rem(step, 8)
    far = lax.div(near + 1, 2)
    shift = sign * (1 - 2 * lax.rem(near + 1, 2)) * far
    mixed = lax.div(step, 8) + near
    return lax.rem(t + shift + 8, 8), mixed


def halves(x):
    high = x.astype(BF16)
    low = (x - high.astype(F32)).astype(BF16)
    return high, low


def builders(
    order_ref, offs_ref, first_ref, second_ref, w_ref, third_ref, fourth_ref,
    c0_ref, c1_ref, w2_ref, w3_ref, u_ref, column_ref, row_ref, pad_ref,
):
    act = lax.axis_index("act")
    first_row = lax.axis_index("wide") * 2
    second_row = lax.axis_index("narrow") * 8
    number = lax.broadcasted_iota(jnp.int32, (16, 256), 0)
    lane = lax.broadcasted_iota(jnp.int32, (16, 256), 1)
    zero = jnp.zeros((16, 256), F32)

    def prepare():
        pad_ref[...] = jnp.zeros_like(pad_ref)
        taps = w_ref[...]
        pad_ref[:, :, 0:65] = taps / jnp.sum(taps, axis=2, keepdims=True)

    def toeplitz(a, d, length, store):
        row = pad_ref[pl.ds(a, 1), d, :]
        shift = lax.rem(offs_ref[d, a] - 32 + 256, 256)
        base = pltpu.roll(jnp.broadcast_to(row, (16, 256)), shift, 1)
        for bit in (1, 2, 4, 8):
            base = jnp.where((number & bit) != 0, pltpu.roll(base, bit, 1), base)
        for start in range(0, length, 16):
            spread = pltpu.roll(base, start, 1) if start else base
            below = jnp.sum(jnp.where(lane >= 192, spread, zero), axis=1, keepdims=True)
            above = jnp.sum(jnp.where((lane >= length) & (lane < 192), spread, zero), axis=1, keepdims=True)
            full = jnp.where(lane == 0, spread + below, jnp.where(lane == length - 1, spread + above, spread))
            full = jnp.where(lane < length, full, zero)
            high = full.astype(BF16).astype(F32)
            store(pl.ds(start, 16), high, full - high)

    def outer(j, carry):
        a = order_ref[j]
        for d, ref in ((0, c0_ref), (1, c1_ref)):

            def store(rows, high, low):
                both = high + pltpu.roll(high, 64, 1) + pltpu.roll(low, 128, 1)
                ref[0, j, rows] = both[:, :128]
                ref[1, j, rows] = both[:, 128:]

            toeplitz(a, d, 64, store)
        return carry

    def inner(j, carry):
        a = order_ref[act * 4 + j]
        for d, ref in ((2, w2_ref), (3, w3_ref)):

            def store(rows, high, low):
                ref[j, rows, 0:128] = high[:, :128].astype(BF16)
                ref[j, rows, 128:256] = high[:, :128].astype(BF16)
                ref[j, rows, 256:384] = low[:, :128].astype(BF16)

            toeplitz(a, d, 128, store)
        column_ref[j] = jnp.broadcast_to(third_ref[pl.ds(a, 1), :], (128, 128)).T
        row_ref[j] = jnp.broadcast_to(fourth_ref[pl.ds(a, 1), :], (8, 128))
        for k in range(16):
            u_ref[j, k] = first_ref[a, first_row + k // 8] + second_ref[a, second_row + k % 8]
        return carry

    return prepare, outer, inner


def stack(x):
    high, low = halves(x)
    return jnp.concatenate([high, low, high, high], axis=0)


def wide_rows(ref, *index):
    return jnp.concatenate([ref[(half,) + index] for half in (0, 1)], axis=-1)


def step_kernel(
    order_ref, offs_ref, cost0_ref, cost1_ref, taps_ref, cost2_ref, cost3_ref, v_ref,
    value_ref, prob_ref,
    c0_ref, c1_ref, w2_ref, w3_ref, u_ref, column_ref, row_ref, pad_ref,
    vt_ref, ga_ref, gb_ref, za_ref, zb_ref, ea_ref, eb_ref, r_ref, score_ref, lse_ref, other_ref,
    first_send, first_recv, first_local, ring_send, ring_recv,
    send_sem, recv_sem, local_sem, lse_send, lse_recv,
):
    y, q, z, act = place()
    wide = 4 * y + q
    row_a = y * 8 + q * 2 + act
    row_b = 64 + z * 8 + q * 2 + act
    barrier = pltpu.get_barrier_semaphore()
    prepare, build_outer, build_inner = builders(
        order_ref, offs_ref, cost0_ref, cost1_ref, taps_ref, cost2_ref, cost3_ref,
        c0_ref, c1_ref, w2_ref, w3_ref, u_ref, column_ref, row_ref, pad_ref,
    )

    def home_a(step):
        t, mixed = partner(step, y, q, 1)
        p = lax.rem(q + lax.rem(lax.div(mixed, 2), 4), 4)
        g = lax.rem(act + lax.rem(mixed, 2), 2)
        return ea_ref.at[4 * t + p, g], {"wide": 4 * t + p, "narrow": z, "act": g}

    def home_b(step):
        t, mixed = partner(step, z, q, -1)
        p = lax.rem(q + lax.rem(lax.div(mixed, 2), 4), 4)
        g = lax.rem(act + lax.rem(mixed, 2), 2)
        return eb_ref.at[t, p, g], {"wide": 4 * y + p, "narrow": t, "act": g}

    def greet(step, carry):
        pl.semaphore_signal(barrier, inc=1, device_id=home_a(step)[1], device_id_type=MESH)
        pl.semaphore_signal(barrier, inc=1, device_id=home_b(step)[1], device_id_type=MESH)
        return carry

    lax.fori_loop(1, 64, greet, 0)

    def pick(n, carry):
        for half in (0, 1):
            vt_ref[half, n] = v_ref[pl.ds(64 * half + 2 * n + act, 16, stride=128), :]
        return carry

    lax.fori_loop(0, 32, pick, 0, unroll=4)
    prepare()
    pl.semaphore_wait(barrier, 126)

    def first(step, carry):
        t, mixed = partner(step, y, q, 1)
        p = lax.rem(q + lax.rem(mixed, 4), 4)
        pltpu.make_async_remote_copy(
            vt_ref.at[0, 4 * t + p],
            ga_ref.at[z, wide],
            first_send.at[0],
            first_recv.at[0],
            {"wide": 4 * t + p, "narrow": z, "act": act},
            MESH,
        ).start()
        t, mixed = partner(step, z, q, -1)
        p = lax.rem(q + lax.rem(mixed, 4), 4)
        pltpu.make_async_remote_copy(
            vt_ref.at[1, 4 * t + p],
            gb_ref.at[y, 4 * z + q],
            first_send.at[1],
            first_recv.at[1],
            {"wide": 4 * y + p, "narrow": t, "act": act},
            MESH,
        ).start()
        return carry

    lax.fori_loop(1, 32, first, 0)
    own = [
        pltpu.make_async_copy(vt_ref.at[0, wide], ga_ref.at[z, wide], first_local.at[0]),
        pltpu.make_async_copy(vt_ref.at[1, 4 * z + q], gb_ref.at[y, 4 * z + q], first_local.at[1]),
    ]
    for copy in own:
        copy.start()
    lax.fori_loop(0, 4, build_outer, 0, unroll=2)
    for copy in own:
        copy.wait()
    streams = (
        (ga_ref, z, lambda t: {"wide": wide, "narrow": t, "act": act}),
        (gb_ref, y, lambda t: {"wide": 4 * t + q, "narrow": z, "act": act}),
    )
    for index, (ref, _, _) in enumerate(streams):
        part = ref.at[0, pl.ds(0, 31)]
        pltpu.make_async_copy(part, part, first_recv.at[index]).wait()

    def hop(index, step, half, way):
        ref, t, device = streams[index]
        block = lax.rem(t + 8 - way * (step - 1), 8)
        piece = ref.at[block, pl.ds(16 * half, 16)]
        side = 0 if way > 0 else 1
        return pltpu.make_async_remote_copy(
            piece,
            piece,
            ring_send.at[index, step - 1, half, side],
            ring_recv.at[index, step - 1, half, side],
            device(lax.rem(t + 8 + way, 8)),
            MESH,
        )

    started = []
    for step in (1, 2, 3, 4):
        for half in (0, 1):
            for index in (0, 1):
                for way in (1, -1):
                    if step == 4 and half != (0 if way > 0 else 1):
                        continue
                    if step > 1:
                        hop(index, step - 1, half, way).wait_recv()
                    copy = hop(index, step, half, way)
                    copy.start()
                    started.append(copy)
        if step == 1:
            lax.fori_loop(4, 8, build_outer, 0, unroll=2)
        if step == 2:
            lax.fori_loop(0, 2, build_inner, 0, unroll=2)
        if step == 3:
            lax.fori_loop(2, 4, build_inner, 0, unroll=2)
    for index in (0, 1):
        hop(index, 3, 1, 1).wait_recv()
        hop(index, 3, 0, -1).wait_recv()
        hop(index, 4, 0, 1).wait_recv()
        hop(index, 4, 1, -1).wait_recv()

    def own_rows(ref, t):
        return wide_rows(ref, slice(None), pl.ds(t * 8, 8)).reshape(64, 256).astype(BF16)

    mine1 = own_rows(c1_ref, z)
    mine0 = own_rows(c0_ref, y)
    gb_rows = gb_ref.reshape(8, 512, 128)

    def first_a(w, carry):
        left = ga_ref[:, w, 0:8, :].reshape(64, 128)
        right = ga_ref[:, w, 8:16, :].reshape(64, 128)
        out = jnp.dot(mine1, stack(jnp.concatenate([left, right], axis=1)), preferred_element_type=F32)
        za_ref[:, pl.ds(16 * w, 8), :] = out[:, :128].reshape(8, 8, 128)
        za_ref[:, pl.ds(16 * w + 8, 8), :] = out[:, 128:].reshape(8, 8, 128)
        return carry


    def first_b(s, carry):
        for i in range(0, 8, 2):
            left = gb_rows[:, pl.ds(64 * s + i, 8, stride=8), :].reshape(64, 128)
            right = gb_rows[:, pl.ds(64 * s + i + 1, 8, stride=8), :].reshape(64, 128)
            out = jnp.dot(mine0, stack(jnp.concatenate([left, right], axis=1)), preferred_element_type=F32)
            zb_ref[pl.ds((8 * s + i) * 64, 64), :] = out[:, :128]
            zb_ref[pl.ds((8 * s + i + 1) * 64, 64), :] = out[:, 128:]
        return carry

    ea_rows = ea_ref.reshape(4096, 128)

    def second_a(part):
        def one(a, carry):
            left = jnp.concatenate([wide_rows(c0_ref, a, pl.ds(half, 32, stride=2)) for half in (0, 1)], axis=0)
            left = left.astype(BF16)
            for i in (0, 2):
                right = jnp.concatenate(
                    [za_ref[a, pl.ds(4 * part + i + k, 64, stride=8), :] for k in range(2)], axis=1
                )
                out = jnp.dot(left, stack(right), preferred_element_type=F32)
                for k in range(2):
                    for half in range(2):
                        start = lax.div(a, 4) * 64 + half * 32 + part * 16 + lax.rem(a, 4) * 4 + i + k
                        ea_rows[pl.ds(start, 32, stride=128), :] = out[
                            32 * half : 32 * half + 32, 128 * k : 128 * k + 128
                        ]
            return carry

        lax.fori_loop(0, 8, one, 0, unroll=2)

    def second_b(half):
        def one(g, carry):
            for a in range(4):
                left = wide_rows(c1_ref, 4 * g + a).astype(BF16)
                for p in (0, 2):
                    start = (4 * g + a) * 8 + 2 * p + half
                    right = jnp.concatenate(
                        [zb_ref[pl.ds(start + 2 * k, 64, stride=64), :] for k in range(2)], axis=1
                    )
                    out = jnp.dot(left, stack(right), preferred_element_type=F32)
                    for k in range(2):
                        block = out[:, 128 * k : 128 * k + 128].reshape(8, 8, 128)
                        for part in range(2):
                            eb_ref[:, p + k, g, 2 * half + part, 4 * a : 4 * a + 4, :] = block[
                                :, 4 * part : 4 * part + 4
                            ]
            return carry

        lax.fori_loop(0, 2, one, 0)

    def send_a(c):
        pltpu.make_async_copy(ea_ref.at[wide, act, c], r_ref.at[c, row_a], local_sem.at[0, c]).start()

        def send(step, carry):
            src, device = home_a(step)
            pltpu.make_async_remote_copy(
                src.at[c], r_ref.at[c, row_a], send_sem.at[0, c], recv_sem.at[0, c], device, MESH
            ).start()
            return carry

        lax.fori_loop(1, 64, send, 0)

    def send_b(c):
        pltpu.make_async_copy(eb_ref.at[z, q, act, c], r_ref.at[c, row_b], local_sem.at[1, c]).start()

        def send(step, carry):
            src, device = home_b(step)
            pltpu.make_async_remote_copy(
                src.at[c], r_ref.at[c, row_b], send_sem.at[1, c], recv_sem.at[1, c], device, MESH
            ).start()
            return carry

        lax.fori_loop(1, 64, send, 0)

    def settle(c, sem):
        for index in (0, 1):
            part = r_ref.at[c, pl.ds(0, 63)]
            pltpu.make_async_copy(part, part, sem.at[index, c]).wait()

    def arrive(c):
        pltpu.make_async_copy(ea_ref.at[wide, act, c], r_ref.at[c, row_a], local_sem.at[0, c]).wait()
        pltpu.make_async_copy(eb_ref.at[z, q, act, c], r_ref.at[c, row_b], local_sem.at[1, c]).wait()
        settle(c, recv_sem)

    def swap(n):
        return pltpu.make_async_remote_copy(
            lse_ref.at[n], other_ref.at[n], lse_send.at[n], lse_recv.at[n], {"act": 1 - act}, MESH
        )

    def compute(n):
        flat = r_ref.at[n // 2].reshape(2048, 128)
        for a in range(4):
            rows = jnp.concatenate(
                [flat[pl.ds(4 * a + 2 * (n % 2) + k, 128, stride=16), :] for k in range(2)], axis=1
            )
            high, low = halves(rows)
            mid = jnp.dot(w2_ref[a], jnp.concatenate([high, low, high], axis=0), preferred_element_type=F32)
            high, low = halves(jnp.concatenate([mid[:, :128], mid[:, 128:]], axis=0))
            expected = lax.dot_general(
                jnp.concatenate([high, low, high], axis=1),
                w3_ref[a],
                (((1,), (1,)), ((), ())),
                preferred_element_type=F32,
            )
            for k in range(2):
                util = (u_ref[a, 2 * n + k] + column_ref[a]) + row_ref[a, 0:1, :]
                score_ref[a, 2 * n + k] = util + DISCOUNT * expected[128 * k : 128 * k + 128]
        for k in range(2):
            scores = [score_ref[a, 2 * n + k] for a in range(4)]
            top = jnp.maximum(jnp.maximum(scores[0], scores[1]), jnp.maximum(scores[2], scores[3]))
            summed = sum(jnp.exp(s - top) for s in scores)
            lse_ref[n, k] = top + jnp.log(summed)

    def finish(n):
        swap(n).wait_recv()
        for k in range(2):
            ours, theirs = lse_ref[n, k], other_ref[n, k]
            top = jnp.maximum(ours, theirs)
            value = top + jnp.log(jnp.exp(ours - top) + jnp.exp(theirs - top))
            value_ref[2 * n + k] = value
            for a in range(4):
                prob_ref[a, 2 * n + k] = jnp.exp(score_ref[a, 2 * n + k] - value).astype(BF16)

    lax.fori_loop(0, 32, first_a, 0, unroll=4)
    second_a(0)
    send_a(0)
    lax.fori_loop(0, 8, first_b, 0)
    second_b(0)
    send_b(0)
    second_a(1)
    send_a(1)
    send_b(1)
    second_b(1)
    for c in (2, 3):
        send_a(c)
        send_b(c)
    for c in range(4):
        arrive(c)
        for n in (2 * c, 2 * c + 1):
            compute(n)
            if n > 0:
                swap(n - 1).start()
            if n > 2:
                finish(n - 3)
    swap(7).start()
    for c in range(4):
        settle(c, send_sem)
    for index, (ref, _, _) in enumerate(streams):
        part = ref.at[0, pl.ds(0, 31)]
        pltpu.make_async_copy(part, part, first_send.at[index]).wait()
    for copy in started:
        copy.wait_send()
    for n in (5, 6, 7):
        finish(n)
    for n in range(8):
        swap(n).wait_send()


def whole(order, offsets, weights, first, second, third, fourth, v):
    dma = pltpu.SemaphoreType.DMA
    return pl.pallas_call(
        step_kernel,
        out_shape=(
            jax.ShapeDtypeStruct((16, 128, 128), F32),
            jax.ShapeDtypeStruct((4, 16, 128, 128), BF16),
        ),
        in_specs=[SMEM] * 4 + [VMEM] * 4,
        out_specs=(VMEM, VMEM),
        scratch_shapes=[
            pltpu.VMEM((2, 8, 64, 128), F32),
            pltpu.VMEM((2, 8, 64, 128), F32),
            pltpu.VMEM((4, 128, 384), BF16),
            pltpu.VMEM((4, 128, 384), BF16),
            pltpu.SMEM((4, 16), F32),
            pltpu.VMEM((4, 128, 128), F32),
            pltpu.VMEM((4, 8, 128), F32),
            pltpu.VMEM((8, 4, 256), F32),
            pltpu.VMEM((2, 32, 16, 128), F32),
            pltpu.VMEM((8, 32, 16, 128), F32),
            pltpu.VMEM((8, 32, 16, 128), F32),
            pltpu.VMEM((8, 512, 128), F32),
            pltpu.VMEM((4096, 128), F32),
            pltpu.VMEM((32, 2, 4, 16, 128), F32),
            pltpu.VMEM((8, 4, 2, 4, 16, 128), F32),
            pltpu.VMEM((4, 128, 16, 128), F32),
            pltpu.VMEM((4, 16, 128, 128), F32),
            pltpu.VMEM((8, 2, 128, 128), F32),
            pltpu.VMEM((8, 2, 128, 128), F32),
            dma((2,)),
            dma((2,)),
            dma((2,)),
            dma((2, 4, 2, 2)),
            dma((2, 4, 2, 2)),
            dma((2, 4)),
            dma((2, 4)),
            dma((2, 4)),
            dma((8,)),
            dma((8,)),
        ],
        compiler_params=pltpu.CompilerParams(collective_id=0, has_side_effects=True, vmem_limit_bytes=LIMIT),
        name="step",
    )(order, offsets.T, first, second, weights, third, fourth, v)


def body(
    value_now,
    cost_first,
    cost_second,
    cost_third,
    cost_fourth,
    trans_weights,
    trans_offsets,
    action_order,
):
    new_value, choice_prob = whole(
        action_order,
        trans_offsets,
        trans_weights,
        cost_first,
        cost_second,
        cost_third,
        cost_fourth,
        value_now.reshape(2048, 128),
    )
    return new_value.reshape(2, 8, 128, 128), choice_prob.reshape(4, 2, 8, 128, 128)


def solution(mesh):
    return jax.shard_map(
        body,
        mesh=mesh,
        in_specs=(P("wide", "narrow", None, None), P(), P(), P(), P(), P(), P(), P()),
        out_specs=(P("wide", "narrow", None, None), P("act", "wide", "narrow", None, None)),
        check_vma=False,
    )
```

time: 511 us -> 137 us (0.27); the launches traced: 501 us -> 136 us
  waiting for transfers between devices: 243 us -> 0 us
  Pallas kernels: 0 us -> 127 us
  blocking collectives: 96.6 us -> 0 us
  matrix products: 55 us -> 0 us
  starting transfers between devices: 31.8 us -> 0 us
  other arithmetic: 26.3 us -> 0 us
  local copies, waits for them, and re-layouts: 33.2 us -> 8.31 us
  between operations: 14.8 us -> 0.66 us
    all_to_all x3 -> x0, waiting for transfers between devices: 166 us -> none  [the longest x1 86.7 us: body(): lax.all_to_all(field, 'wide', split_axis=3, concat_axis=1, tiled=True)]
    pallas_call x0 -> x1, Pallas kernels: none -> 127 us  [whole(): pl.pallas_call(step_kernel, out_shape=(jax.ShapeDtypeStruct((16, 128, 128...]
    all_to_all x1 -> x0, blocking collectives: 96.6 us -> none  [body(): lax.all_to_all(field, 'narrow', split_axis=2, concat_axis=3, tiled=True)]
    all_gather x2 -> x0, waiting for transfers between devices: 77.5 us -> none  [merged(): pieces = jax.tree.map(lambda part: lax.all_gather(part, axis), value)]
    dot_general x8 -> x0, matrix products: 55 us -> none  [the longest x4 32.7 us: transition(): return jnp.einsum('ijk,j->ik', matched, normed, precision=HIGHEST)]
    all_to_all x3 -> x0, starting transfers between devices: 31.7 us -> none  [the longest x1 13.2 us: body(): lax.all_to_all(field, 'wide', split_axis=3, concat_axis=1, tiled=True)]
    eq x2 -> x0, other arithmetic: 13.6 us -> none  [transition(): target[:, :, None] == row_ids[None, None, :]]
    all_to_all x6 -> x0, local copies, waits for them, and re-layouts: 13.1 us -> none  [the longest x2 5.01 us: body(): lax.all_to_all(field, 'narrow', split_axis=2, concat_axis=3, tiled=True)]
  transfers between devices with their start and end apart: 5 -> 0, of which waited for: 5 -> 0; matrix products, arithmetic and copies ran while one was open for 11% -> 0% of each run, Pallas kernels for 0% -> 0%
where the time goes in v3:
time: 137 us; the launch traced here: 136 us
  Pallas kernels  127 us (93%)
  local copies, waits for them, and re-layouts  8.31 us (6%)
    pallas_call x1, Pallas kernels, whole(): pl.pallas_call(step_kernel, out_shape=(jax.ShapeDtypeStruct((16, 128, 128...  127 us
    unnamed x18, local copies, waits for them, and re-layouts  8.31 us

profile of v3, /device:TPU:1, one launch (start us, length us, event | category | flops | bytes accessed | tf_op | source)
XLA Modules:
  0.0 136.2 jit_solution(4582433129260442560)
XLA Ops:
  0.6 0.0 copy-start
  0.6 1.2 copy-done
  1.9 0.0 copy-start.1
  1.9 0.7 copy-done.1
  2.6 0.0 copy-start.2
  2.6 0.7 copy-done.2
  3.3 0.0 copy-start.3
  3.3 0.7 copy-done.3
  4.0 0.0 copy-start.4
  4.0 0.7 copy-done.4
  4.6 0.0 copy-start.5
  4.6 0.7 copy-done.5
  5.3 0.0 copy-start.6
  5.3 0.7 copy-done.6
  6.0 0.0 copy-start.7
  6.0 0.7 copy-done.7
  6.7 127.3 %step.1 = (f32[16,128,128]{2,1,0:T(8,128)S(1)}, bf16[4,16,128,128]{3,2,1,0:T(8,128)(2,1)S(1)}) custom-call(s32[8]{0:T(128)S(1)} %copy-done.7, s32[4,8]{1,0:T(4,128)S(1)} %bitcast.7, f32[8,64]{1,0:T(8,128)S(1)} %copy-done.2, f32[8,64]{1,0:T(8,128)S(1)} %copy-done.3, f32[8,4,65]{2,1,0:T(4,128)S(1)} %copy-done.1, f32[8,128]{1,0:T(8,128)S(1)} %copy-done.4, ...), custom_call_target="tpu_custom_call" | custom-call | tf_op jit(solution)/shard_map/step/pallas_call | solution.py:408
  133.9 1.0 copy.12
  134.9 1.3 copy.13
Async XLA Ops:
  0.6 1.2 copy-start
  1.9 0.7 copy-start.1
  2.6 0.7 copy-start.2
  3.3 0.7 copy-start.3
  4.0 0.7 copy-start.4
  4.6 0.7 copy-start.5
  5.3 0.7 copy-start.6
  6.0 0.7 copy-start.7

commit v4 on v3

--- a/solution.py
+++ b/solution.py
@@ -11,7 +11,7 @@
 BF16 = jnp.bfloat16
 VMEM = pl.BlockSpec(memory_space=pltpu.VMEM)
 SMEM = pl.BlockSpec(memory_space=pltpu.SMEM)
-LIMIT = 34 * 1024 * 1024
+LIMIT = 56 * 1024 * 1024
 
 
 def place():
@@ -105,8 +105,10 @@
 
 
 def step_kernel(
-    order_ref, offs_ref, cost0_ref, cost1_ref, taps_ref, cost2_ref, cost3_ref, v_ref,
-    value_ref, prob_ref,
+    order_in, offs_in, cost0_in, cost1_in, taps_in, cost2_in, cost3_in, v_in,
+    value_out, prob_out,
+    value_ref, prob_ref, store_sem,
+    order_ref, offs_ref, cost0_ref, cost1_ref, taps_ref, cost2_ref, cost3_ref, v_ref, load_sem,
     c0_ref, c1_ref, w2_ref, w3_ref, u_ref, column_ref, row_ref, pad_ref,
     vt_ref, ga_ref, gb_ref, za_ref, zb_ref, ea_ref, eb_ref, r_ref, score_ref, lse_ref, other_ref,
     first_send, first_recv, first_local, ring_send, ring_recv,
@@ -117,6 +119,23 @@
     row_a = y * 8 + q * 2 + act
     row_b = 64 + z * 8 + q * 2 + act
     barrier = pltpu.get_barrier_semaphore()
+    loads = [
+        pltpu.make_async_copy(src, dst, load_sem.at[n])
+        for n, (src, dst) in enumerate(
+            (
+                (v_in, v_ref),
+                (taps_in, taps_ref),
+                (order_in, order_ref),
+                (offs_in, offs_ref),
+                (cost0_in, cost0_ref),
+                (cost1_in, cost1_ref),
+                (cost2_in, cost2_ref),
+                (cost3_in, cost3_ref),
+            )
+        )
+    ]
+    for load in loads:
+        load.start()
     prepare, build_outer, build_inner = builders(
         order_ref, offs_ref, cost0_ref, cost1_ref, taps_ref, cost2_ref, cost3_ref,
         c0_ref, c1_ref, w2_ref, w3_ref, u_ref, column_ref, row_ref, pad_ref,
@@ -139,7 +158,9 @@
         pl.semaphore_signal(barrier, inc=1, device_id=home_b(step)[1], device_id_type=MESH)
         return carry
 
-    lax.fori_loop(1, 64, greet, 0)
+    lax.fori_loop(1, 64, greet, 0, unroll=3)
+    for load in loads:
+        load.wait()
 
     def pick(n, carry):
         for half in (0, 1):
@@ -305,7 +326,7 @@
             ).start()
             return carry
 
-        lax.fori_loop(1, 64, send, 0)
+        lax.fori_loop(1, 64, send, 0, unroll=3)
 
     def send_b(c):
         pltpu.make_async_copy(eb_ref.at[z, q, act, c], r_ref.at[c, row_b], local_sem.at[1, c]).start()
@@ -317,7 +338,7 @@
             ).start()
             return carry
 
-        lax.fori_loop(1, 64, send, 0)
+        lax.fori_loop(1, 64, send, 0, unroll=3)
 
     def settle(c, sem):
         for index in (0, 1):
@@ -387,9 +408,19 @@
             compute(n)
             if n > 0:
                 swap(n - 1).start()
-            if n > 2:
-                finish(n - 3)
     swap(7).start()
+
+    def stores(n):
+        rows = pl.ds(2 * n, 2)
+        return (
+            pltpu.make_async_copy(value_ref.at[rows], value_out.at[rows], store_sem.at[0, n]),
+            pltpu.make_async_copy(prob_ref.at[:, rows], prob_out.at[:, rows], store_sem.at[1, n]),
+        )
+
+    for n in range(8):
+        finish(n)
+        for copy in stores(n):
+            copy.start()
     for c in range(4):
         settle(c, send_sem)
     for index, (ref, _, _) in enumerate(streams):
@@ -397,10 +428,11 @@
         pltpu.make_async_copy(part, part, first_send.at[index]).wait()
     for copy in started:
         copy.wait_send()
-    for n in (5, 6, 7):
-        finish(n)
     for n in range(8):
         swap(n).wait_send()
+    for n in range(8):
+        for copy in stores(n):
+            copy.wait()
 
 
 def whole(order, offsets, weights, first, second, third, fourth, v):
@@ -411,9 +443,21 @@
             jax.ShapeDtypeStruct((16, 128, 128), F32),
             jax.ShapeDtypeStruct((4, 16, 128, 128), BF16),
         ),
-        in_specs=[SMEM] * 4 + [VMEM] * 4,
-        out_specs=(VMEM, VMEM),
+        in_specs=[pl.BlockSpec(memory_space=pltpu.HBM)] * 8,
+        out_specs=(pl.BlockSpec(memory_space=pltpu.HBM),) * 2,
         scratch_shapes=[
+            pltpu.VMEM((16, 128, 128), F32),
+            pltpu.VMEM((4, 16, 128, 128), BF16),
+            dma((2, 8)),
+            pltpu.SMEM((8,), jnp.int32),
+            pltpu.SMEM((4, 8), jnp.int32),
+            pltpu.SMEM((8, 64), F32),
+            pltpu.SMEM((8, 64), F32),
+            pltpu.VMEM((8, 4, 65), F32),
+            pltpu.VMEM((8, 128), F32),
+            pltpu.VMEM((8, 128), F32),
+            pltpu.VMEM((2048, 128), F32),
+            dma((8,)),
             pltpu.VMEM((2, 8, 64, 128), F32),
             pltpu.VMEM((2, 8, 64, 128), F32),
             pltpu.VMEM((4, 128, 384), BF16),

time: 137 us -> 131 us (0.956)
  local copies, waits for them, and re-layouts: 8.31 us -> 3.77 us
    unnamed x18 -> x4, local copies, waits for them, and re-layouts: 8.31 us -> 3.77 us
where the time goes in v4:
time: 131 us
  Pallas kernels  127 us (97%)
  local copies, waits for them, and re-layouts  3.77 us (3%)
    pallas_call x1, Pallas kernels, whole(): pl.pallas_call(step_kernel, out_shape=(jax.ShapeDtypeStruct((16, 128, 128...  127 us
    unnamed x4, local copies, waits for them, and re-layouts  3.77 us

profile of v4, /device:TPU:1, one launch (start us, length us, event | category | flops | bytes accessed | tf_op | source)
XLA Modules:
  0.0 131.3 jit_solution(11223357596403751401)
XLA Ops:
  0.6 126.9 %step.1 = (f32[16,128,128]{2,1,0:T(8,128)}, bf16[4,16,128,128]{3,2,1,0:T(8,128)(2,1)}) custom-call(s32[8]{0:T(128)} %order_in.1, s32[4,8]{1,0:T(4,128)} %bitcast.7, f32[8,64]{1,0:T(8,128)} %cost0_in.1, f32[8,64]{1,0:T(8,128)} %cost1_in.1, f32[8,4,65]{2,1,0:T(4,128)} %taps_in.1, f32[8,128]{1,0:T(8,128)} %cost2_in.1, f32[8,128]{1,0:T(8,128)} %cost3_in.1, ...), custom_call_target="tpu_custom_call" | custom-call | tf_op jit(solution)/shard_map/step/pallas_call | solution.py:440
  127.6 0.0 copy-start
  127.6 2.4 %copy.12 = f32[2,8,128,128]{3,2,1,0:T(8,128)} copy(f32[2,8,128,128]{3,2,1,0:T(8,128)} %bitcast.6) | data formatting | bytes 2097152
  130.0 0.0 copy-done
  130.0 1.3 %copy.13 = bf16[4,2,8,128,128]{4,3,2,1,0:T(8,128)(2,1)} copy(bf16[4,2,8,128,128]{4,3,2,1,0:T(8,128)(2,1)S(1)} %bitcast.4) | data formatting | bytes 4194304
Async XLA Ops:
  127.6 2.5 %copy-start = (bf16[4,16,128,128]{3,2,1,0:T(8,128)(2,1)S(1)}, bf16[4,16,128,128]{3,2,1,0:T(8,128)(2,1)}, u32[]{:S(2)}) copy-start(bf16[4,16,128,128]{3,2,1,0:T(8,128)(2,1)} %get-tuple-element.5) | copy-start | bytes 6291460

commit v5 on v4

--- a/solution.py
+++ b/solution.py
@@ -194,7 +194,7 @@
         ).start()
         return carry
 
-    lax.fori_loop(1, 32, first, 0)
+    lax.fori_loop(1, 32, first, 0, unroll=2)
     own = [
         pltpu.make_async_copy(vt_ref.at[0, wide], ga_ref.at[z, wide], first_local.at[0]),
         pltpu.make_async_copy(vt_ref.at[1, 4 * z + q], gb_ref.at[y, 4 * z + q], first_local.at[1]),
@@ -244,7 +244,8 @@
             lax.fori_loop(0, 2, build_inner, 0, unroll=2)
         if step == 3:
             lax.fori_loop(2, 4, build_inner, 0, unroll=2)
-    for index in (0, 1):
+
+    def gathered(index):
         hop(index, 3, 1, 1).wait_recv()
         hop(index, 3, 0, -1).wait_recv()
         hop(index, 4, 0, 1).wait_recv()
@@ -316,39 +317,51 @@
 
         lax.fori_loop(0, 2, one, 0)
 
-    def send_a(c):
-        pltpu.make_async_copy(ea_ref.at[wide, act, c], r_ref.at[c, row_a], local_sem.at[0, c]).start()
+    groups = (pl.ds(0, 2), 2, 3)
+
+    def local_a(m):
+        c = groups[m]
+        return pltpu.make_async_copy(ea_ref.at[wide, act, c], r_ref.at[c, row_a], local_sem.at[0, m])
+
+    def local_b(m):
+        c = groups[m]
+        return pltpu.make_async_copy(eb_ref.at[z, q, act, c], r_ref.at[c, row_b], local_sem.at[1, m])
+
+    def send_a(m):
+        c = groups[m]
+        local_a(m).start()
 
         def send(step, carry):
             src, device = home_a(step)
             pltpu.make_async_remote_copy(
-                src.at[c], r_ref.at[c, row_a], send_sem.at[0, c], recv_sem.at[0, c], device, MESH
+                src.at[c], r_ref.at[c, row_a], send_sem.at[0, m], recv_sem.at[0, m], device, MESH
             ).start()
             return carry
 
         lax.fori_loop(1, 64, send, 0, unroll=3)
 
-    def send_b(c):
-        pltpu.make_async_copy(eb_ref.at[z, q, act, c], r_ref.at[c, row_b], local_sem.at[1, c]).start()
+    def send_b(m):
+        c = groups[m]
+        local_b(m).start()
 
         def send(step, carry):
             src, device = home_b(step)
             pltpu.make_async_remote_copy(
-                src.at[c], r_ref.at[c, row_b], send_sem.at[1, c], recv_sem.at[1, c], device, MESH
+                src.at[c], r_ref.at[c, row_b], send_sem.at[1, m], recv_sem.at[1, m], device, MESH
             ).start()
             return carry
 
         lax.fori_loop(1, 64, send, 0, unroll=3)
 
-    def settle(c, sem):
+    def settle(m, sem):
         for index in (0, 1):
-            part = r_ref.at[c, pl.ds(0, 63)]
-            pltpu.make_async_copy(part, part, sem.at[index, c]).wait()
-
-    def arrive(c):
-        pltpu.make_async_copy(ea_ref.at[wide, act, c], r_ref.at[c, row_a], local_sem.at[0, c]).wait()
-        pltpu.make_async_copy(eb_ref.at[z, q, act, c], r_ref.at[c, row_b], local_sem.at[1, c]).wait()
-        settle(c, recv_sem)
+            part = r_ref.at[groups[m], pl.ds(0, 63)]
+            pltpu.make_async_copy(part, part, sem.at[index, m]).wait()
+
+    def arrive(m):
+        local_a(m).wait()
+        local_b(m).wait()
+        settle(m, recv_sem)
 
     def swap(n):
         return pltpu.make_async_remote_copy(
@@ -389,22 +402,22 @@
             for a in range(4):
                 prob_ref[a, 2 * n + k] = jnp.exp(score_ref[a, 2 * n + k] - value).astype(BF16)
 
-    lax.fori_loop(0, 32, first_a, 0, unroll=4)
-    second_a(0)
-    send_a(0)
+    gathered(1)
     lax.fori_loop(0, 8, first_b, 0)
     second_b(0)
     send_b(0)
+    gathered(0)
+    lax.fori_loop(0, 32, first_a, 0, unroll=4)
+    second_a(0)
     second_a(1)
-    send_a(1)
-    send_b(1)
+    send_a(0)
     second_b(1)
-    for c in (2, 3):
-        send_a(c)
-        send_b(c)
-    for c in range(4):
-        arrive(c)
-        for n in (2 * c, 2 * c + 1):
+    for m in (1, 2):
+        send_a(m)
+        send_b(m)
+    for m, pieces in enumerate(((0, 1, 2, 3), (4, 5), (6, 7))):
+        arrive(m)
+        for n in pieces:
             compute(n)
             if n > 0:
                 swap(n - 1).start()
@@ -421,8 +434,8 @@
         finish(n)
         for copy in stores(n):
             copy.start()
-    for c in range(4):
-        settle(c, send_sem)
+    for m in range(3):
+        settle(m, send_sem)
     for index, (ref, _, _) in enumerate(streams):
         part = ref.at[0, pl.ds(0, 31)]
         pltpu.make_async_copy(part, part, first_send.at[index]).wait()
@@ -482,9 +495,9 @@
             dma((2,)),
             dma((2, 4, 2, 2)),
             dma((2, 4, 2, 2)),
-            dma((2, 4)),
-            dma((2, 4)),
-            dma((2, 4)),
+            dma((2, 3)),
+            dma((2, 3)),
+            dma((2, 3)),
             dma((8,)),
             dma((8,)),
         ],

time: 131 us -> 131 us (level)
  no operation moved by 1% of the time
where the time goes in v5:
time: 131 us
  Pallas kernels  126 us (96%)
  local copies, waits for them, and re-layouts  3.77 us (3%)
    pallas_call x1, Pallas kernels, whole(): pl.pallas_call(step_kernel, out_shape=(jax.ShapeDtypeStruct((16, 128, 128...  126 us
    unnamed x4, local copies, waits for them, and re-layouts  3.77 us

profile of v5, /device:TPU:1, one launch (start us, length us, event | category | flops | bytes accessed | tf_op | source)
XLA Modules:
  0.0 130.6 jit_solution(2804626702102264534)
XLA Ops:
  0.6 126.2 %step.1 = (f32[16,128,128]{2,1,0:T(8,128)}, bf16[4,16,128,128]{3,2,1,0:T(8,128)(2,1)}) custom-call(s32[8]{0:T(128)} %order_in.1, s32[4,8]{1,0:T(4,128)} %bitcast.7, f32[8,64]{1,0:T(8,128)} %cost0_in.1, f32[8,64]{1,0:T(8,128)} %cost1_in.1, f32[8,4,65]{2,1,0:T(4,128)} %taps_in.1, f32[8,128]{1,0:T(8,128)} %cost2_in.1, f32[8,128]{1,0:T(8,128)} %cost3_in.1, ...), custom_call_target="tpu_custom_call" | custom-call | tf_op jit(solution)/shard_map/step/pallas_call | solution.py:453
  126.9 0.0 copy-start
  126.9 2.4 %copy.12 = f32[2,8,128,128]{3,2,1,0:T(8,128)} copy(f32[2,8,128,128]{3,2,1,0:T(8,128)} %bitcast.6) | data formatting | bytes 2097152
  129.3 0.0 copy-done
  129.3 1.3 %copy.13 = bf16[4,2,8,128,128]{4,3,2,1,0:T(8,128)(2,1)} copy(bf16[4,2,8,128,128]{4,3,2,1,0:T(8,128)(2,1)S(1)} %bitcast.4) | data formatting | bytes 4194304
Async XLA Ops:
  126.9 2.5 %copy-start = (bf16[4,16,128,128]{3,2,1,0:T(8,128)(2,1)S(1)}, bf16[4,16,128,128]{3,2,1,0:T(8,128)(2,1)}, u32[]{:S(2)}) copy-start(bf16[4,16,128,128]{3,2,1,0:T(8,128)(2,1)} %get-tuple-element.5) | copy-start | bytes 6291460

commit v6 on v5

--- a/solution.py
+++ b/solution.py
@@ -11,7 +11,7 @@
 BF16 = jnp.bfloat16
 VMEM = pl.BlockSpec(memory_space=pltpu.VMEM)
 SMEM = pl.BlockSpec(memory_space=pltpu.SMEM)
-LIMIT = 56 * 1024 * 1024
+LIMIT = 36 * 1024 * 1024
 
 
 def place():
@@ -368,7 +368,7 @@
             lse_ref.at[n], other_ref.at[n], lse_send.at[n], lse_recv.at[n], {"act": 1 - act}, MESH
         )
 
-    def compute(n):
+    def compute(n, between=None):
         flat = r_ref.at[n // 2].reshape(2048, 128)
         for a in range(4):
             rows = jnp.concatenate(
@@ -386,6 +386,8 @@
             for k in range(2):
                 util = (u_ref[a, 2 * n + k] + column_ref[a]) + row_ref[a, 0:1, :]
                 score_ref[a, 2 * n + k] = util + DISCOUNT * expected[128 * k : 128 * k + 128]
+            if a == 0 and between is not None:
+                between()
         for k in range(2):
             scores = [score_ref[a, 2 * n + k] for a in range(4)]
             top = jnp.maximum(jnp.maximum(scores[0], scores[1]), jnp.maximum(scores[2], scores[3]))
@@ -418,9 +420,7 @@
     for m, pieces in enumerate(((0, 1, 2, 3), (4, 5), (6, 7))):
         arrive(m)
         for n in pieces:
-            compute(n)
-            if n > 0:
-                swap(n - 1).start()
+            compute(n, swap(n - 1).start if n > 0 else None)
     swap(7).start()
 
     def stores(n):
@@ -450,6 +450,7 @@
 
 def whole(order, offsets, weights, first, second, third, fourth, v):
     dma = pltpu.SemaphoreType.DMA
+    operands = (order, offsets.T, first, second, weights, third, fourth, v)
     return pl.pallas_call(
         step_kernel,
         out_shape=(
@@ -457,7 +458,7 @@
             jax.ShapeDtypeStruct((4, 16, 128, 128), BF16),
         ),
         in_specs=[pl.BlockSpec(memory_space=pltpu.HBM)] * 8,
-        out_specs=(pl.BlockSpec(memory_space=pltpu.HBM),) * 2,
+        out_specs=(pl.BlockSpec(memory_space=pl.ANY),) * 2,
         scratch_shapes=[
             pltpu.VMEM((16, 128, 128), F32),
             pltpu.VMEM((4, 16, 128, 128), BF16),
@@ -503,7 +504,7 @@
         ],
         compiler_params=pltpu.CompilerParams(collective_id=0, has_side_effects=True, vmem_limit_bytes=LIMIT),
         name="step",
-    )(order, offsets.T, first, second, weights, third, fourth, v)
+    )(*(pltpu.with_memory_space_constraint(x, pltpu.HBM) for x in operands))
 
 
 def body(

time: 131 us -> 128 us (0.977)
  local copies, waits for them, and re-layouts: 3.77 us -> 2.29 us
    unnamed x4 -> x2, local copies, waits for them, and re-layouts: 3.77 us -> 2.29 us
where the time goes in v6:
time: 128 us
  Pallas kernels  125 us (98%)
  local copies, waits for them, and re-layouts  2.29 us (2%)
    pallas_call x1, Pallas kernels, whole(): pl.pallas_call(step_kernel, out_shape=(jax.ShapeDtypeStruct((16, 128, 128...  125 us

profile of v6, /device:TPU:1, one launch (start us, length us, event | category | flops | bytes accessed | tf_op | source)
XLA Modules:
  0.0 128.2 jit_solution(390694695428971377)
XLA Ops:
  0.6 125.3 %step.1 = (f32[16,128,128]{2,1,0:T(8,128)S(1)}, bf16[4,16,128,128]{3,2,1,0:T(8,128)(2,1)S(1)}) custom-call(s32[8]{0:T(128)} %order_in.1, s32[4,8]{1,0:T(4,128)} %bitcast.7, f32[8,64]{1,0:T(8,128)} %cost0_in.1, f32[8,64]{1,0:T(8,128)} %cost1_in.1, f32[8,4,65]{2,1,0:T(4,128)} %taps_in.1, f32[8,128]{1,0:T(8,128)} %cost2_in.1, f32[8,128]{1,0:T(8,128)} %cost3_in.1, ...), custom_call_target="tpu_custom_call" | custom-call | tf_op jit(solution)/shard_map/step/pallas_call | solution.py:454
  125.9 1.0 copy.12
  126.9 1.3 %copy.13 = bf16[4,2,8,128,128]{4,3,2,1,0:T(8,128)(2,1)} copy(bf16[4,2,8,128,128]{4,3,2,1,0:T(8,128)(2,1)S(1)} %bitcast.4) | data formatting | bytes 4194304
